TPU v7x, 512 devices: a whole 4x8x8 slice. The times are simulated.
512 devices in a mesh: tile: 64 (over z, x, core), lev: 8 (over y).
Axes of the slice: x: 4, y: 8, z: 8, core: 2. Of those that a mesh axis runs over, the one named last changes fastest.
Arguments:
- tracers: bfloat16 [8, 32, 1024, 128], P(None, 'lev', 'tile'), may hold values from -6 to 6
- wind_field: bfloat16 [3, 32, 1024, 128], P(None, 'lev', 'tile'), may hold values from -5 to 5
- regions: int32 [4, 1024, 2], P(None, 'tile'), may hold values from 0 to 62, as said below
- stencil_base: int32 [4, 2, 1024, 128], P(None, None, 'tile'), may hold values from 0 to 28, as said below
- far_start: int32 [4, 64, 2], replicated, may hold values from 0 to 15, as said below
Outputs:
- tracers_new: bfloat16 [8, 32, 1024, 128], P(None, 'lev', 'tile')
- displacement: float32 [3, 32, 1024, 128], P(None, 'lev', 'tile')
Inputs may be any that keep to these rules, and one draw needn't show every extreme that they name: For an arrival block of band r, regions[k, j, 0] lies in r - 2 to r + 1 and in 0 to 62, and regions[k, j, 1] in 0 to 15. Every column that band r's patches at section k take from band r - 2 lies in the cyclic run of 8 columns from far_start[k, r - 2, 0], and every column taken from band r + 2 in the run from far_start[k, r + 2, 1]. stencil_base[k, 0] is at most 28 and stencil_base[k, 1] at most 12.
All inputs are finite; a program needn't handle non-finite values.
Results may differ from a plain program's by a relative error of at most 0.001.
Values may be sent and summed in bfloat16 or wider, within the bound.
No kernel may reach another device: no remote copies, remote signals or barrier semaphores. Data moves between devices by JAX's collectives and lax.ppermute only.
A program may use at most 64 MiB of HBM per device.

v0:
```python
import jax
import jax.numpy as jnp
from jax import lax
from jax.experimental import pallas as pl
from jax.experimental.pallas import tpu as pltpu
from jax.sharding import PartitionSpec as P

ITERS = 3
BW = 16
BH = 8
CELLS = BW * BH
QUADS = 4
POINTS = QUADS * CELLS
N_OFF = 5


def shifted(shard, axis, by):
    devices = lax.axis_size(axis)
    pairs = [(i, i + by) for i in range(devices) if 0 <= i + by < devices]
    return lax.ppermute(shard, axis, pairs)


def lagrange_cubic(position):
    return [
        -(position - 1.0) * (position - 2.0) * (position - 3.0) / 6.0,
        position * (position - 2.0) * (position - 3.0) / 2.0,
        -position * (position - 1.0) * (position - 3.0) / 2.0,
        position * (position - 1.0) * (position - 2.0) / 6.0,
    ]


def selectors(regions, own_band, start_low, start_high, nblocks):
    upper = regions[:, 0:1]
    left = regions[:, 1:2]
    lane = lax.broadcasted_iota(jnp.int32, (nblocks, N_OFF * nblocks), 1)
    rows = []
    for quad_y in (0, 1):
        for quad_x in (0, 1):
            offset = upper + (quad_y - own_band)
            col = (left + quad_x) & (nblocks - 1)
            run_low = (col - start_low) & (nblocks - 1)
            run_high = (col - start_high) & (nblocks - 1)
            run = jnp.where(offset == -2, run_low, jnp.where(offset == 2, run_high, 0))
            slot = jnp.where(run < nblocks // 2, (offset + 2) * nblocks + col, -1)
            rows.append(jnp.where(lane == slot, 1.0, 0.0).astype(jnp.bfloat16))
    return jnp.concatenate(rows, axis=0)


def class_order(log_step):
    step = 1 << log_step
    mask = step - 1
    source = lax.broadcasted_iota(jnp.int32, (POINTS, 128), 0)
    lane = lax.broadcasted_iota(jnp.int32, (POINTS, 128), 1)
    x = (source & (BW - 1)) + ((source >> 7) & 1) * BW
    y = ((source >> 4) & (BH - 1)) + (source >> 8) * BH
    kind = (y & mask) * step + (x & mask)
    place = (y >> log_step) * (2 * BW // step) + (x >> log_step)
    dest = kind * (POINTS // (step * step)) + place
    cols = [
        jnp.where(dest == lane + v * 128, 1.0, 0.0).astype(jnp.bfloat16) for v in range(QUADS)
    ]
    return jnp.concatenate(cols, axis=1)


def sort_rows(picked, nblocks, lanes_at):
    return jnp.concatenate(
        [
            picked[q * nblocks : (q + 1) * nblocks, lanes_at : lanes_at + CELLS]
            for q in range(QUADS)
        ],
        axis=1,
    )


def take_lanes(values, index):
    return jnp.take_along_axis(values, index, axis=1, mode="promise_in_bounds")


def wind_kernel(
    own_ref, far_ref, regions_ref, base_ref, lo2, lo1, mid, hi1, hi2, out_ref, rows_ref, patch_ref
):
    n_comp, n_level, nblocks, _ = out_ref.shape
    n_bands = far_ref.shape[1]
    own = own_ref[0]
    low_at = jnp.maximum(own - 2, 0)
    high_at = jnp.minimum(own + 2, n_bands - 1)
    pick = jnp.concatenate(
        [
            selectors(regions_ref[k], own, far_ref[k, low_at, 0], far_ref[k, high_at, 1], nblocks)
            for k in range(ITERS)
        ],
        axis=0,
    )
    bands = (lo2, lo1, mid, hi1, hi2)
    fields = [(c, l) for c in range(n_comp) for l in range(n_level)]
    for i in range(0, len(fields), 2):
        pair = [
            jnp.concatenate([b[c, l] for b in bands], axis=0) for c, l in fields[i : i + 2]
        ]
        picked = jnp.dot(
            pick, jnp.concatenate(pair, axis=1), preferred_element_type=jnp.float32
        ).astype(jnp.bfloat16)
        for k in range(ITERS):
            part = picked[k * QUADS * nblocks : (k + 1) * QUADS * nblocks]
            for half in range(2):
                at = (k * len(fields) + i + half) * nblocks
                rows_ref[at : at + nblocks, :] = sort_rows(part, nblocks, half * CELLS)
    patch_ref[...] = jnp.dot(rows_ref[...], class_order(1), preferred_element_type=jnp.float32)
    for h in range(0, nblocks, 8):
        displace = None
        for k in range(ITERS):
            x0 = base_ref[k, 0, h : h + 8, :] + 1
            y0 = base_ref[k, 1, h : h + 8, :] + 1
            xs = [(x0 + 1) >> 1, x0 >> 1]
            ys = [((y0 + 1) >> 1) * BW, (y0 >> 1) * BW]
            index = [[ys[ry] + xs[rx] for rx in range(2)] for ry in range(2)]
            odd_x = (x0 & 1) == 1
            odd_y = (y0 & 1) == 1
            after = []
            for l in range(n_level):
                if displace is None:
                    frac_x = jnp.full(x0.shape, 0.5, jnp.float32)
                    frac_y = frac_x
                else:
                    frac_x = 0.5 + 0.5 * jnp.tanh(displace[l][0])
                    frac_y = 0.5 + 0.5 * jnp.tanh(displace[l][1])
                weight_x = [
                    jnp.where(odd_x, frac_x, 1.0 - frac_x),
                    jnp.where(odd_x, 1.0 - frac_x, frac_x),
                ]
                weight_y = [
                    jnp.where(odd_y, frac_y, 1.0 - frac_y),
                    jnp.where(odd_y, 1.0 - frac_y, frac_y),
                ]
                weight = [[weight_x[rx] * weight_y[ry] for rx in range(2)] for ry in range(2)]
                comps = []
                for c in range(n_comp):
                    at = (k * len(fields) + c * n_level + l) * nblocks + h
                    total = None
                    for ry in range(2):
                        for rx in range(2):
                            kind = ry * 2 + rx
                            values = patch_ref[at : at + 8, kind * 128 : (kind + 1) * 128]
                            term = weight[ry][rx] * take_lanes(values, index[ry][rx])
                            total = term if total is None else total + term
                    arrive = mid[c, l, h : h + 8, :].astype(jnp.float32)
                    comps.append(0.5 * (arrive + total))
                after.append(comps)
            displace = after
        for l in range(n_level):
            for c in range(n_comp):
                out_ref[c, l, h : h + 8, :] = displace[l][c]


def tracer_kernel(
    own_ref,
    far_ref,
    regions_ref,
    base_ref,
    displace_ref,
    below_ref,
    above_ref,
    lo2,
    lo1,
    mid,
    hi1,
    hi2,
    out_ref,
    rows_ref,
    patch_ref,
    weight_ref,
):
    n_tracer, n_level, nblocks, _ = out_ref.shape
    n_ext = n_level + 2
    n_bands = far_ref.shape[1]
    first = lo2.shape[0] - n_tracer
    own = own_ref[0]
    at_bottom = own_ref[1] == 0
    at_top = own_ref[1] == own_ref[2] - 1
    low_at = jnp.maximum(own - 2, 0)
    high_at = jnp.minimum(own + 2, n_bands - 1)
    k = ITERS
    pick = selectors(regions_ref[k], own, far_ref[k, low_at, 0], far_ref[k, high_at, 1], nblocks)
    bands = (lo2, lo1, mid, hi1, hi2)
    for t in range(n_tracer):
        levels = [
            jnp.concatenate([b[first + t, l] for b in bands], axis=0) for l in range(n_level)
        ]
        bottom = jnp.where(at_bottom, levels[0], below_ref[t])
        top = jnp.where(at_top, levels[-1], above_ref[t])
        levels = [bottom] + levels + [top]
        for e in range(0, n_ext, 2):
            picked = jnp.dot(
                pick,
                jnp.concatenate(levels[e : e + 2], axis=1),
                preferred_element_type=jnp.float32,
            ).astype(jnp.bfloat16)
            for half in range(2):
                at = (t * n_ext + e + half) * nblocks
                rows_ref[at : at + nblocks, :] = sort_rows(picked, nblocks, half * CELLS)
    patch_ref[...] = jnp.dot(rows_ref[...], class_order(2), preferred_element_type=jnp.float32)
    for h in range(0, nblocks, 8):
        x0 = base_ref[k, 0, h : h + 8, :]
        y0 = base_ref[k, 1, h : h + 8, :]
        xs = [((x0 + ((r - x0) & 3)) >> 2) + r * 32 for r in range(4)]
        ys = [((y0 + ((r - y0) & 3)) >> 2) * 8 for r in range(4)]
        index = [[ys[ry] + xs[rx] for rx in range(4)] for ry in range(4)]
        layers = []
        for l in range(n_level):
            split = []
            for axis, start in ((0, x0), (1, y0)):
                w = lagrange_cubic(1.5 + 0.5 * jnp.tanh(displace_ref[axis, l, h : h + 8, :]))
                bit0 = (start & 1) == 1
                bit1 = (start & 2) == 2
                w = [jnp.where(bit0, w[(r - 1) & 3], w[r]) for r in range(4)]
                w = [jnp.where(bit1, w[(r - 2) & 3], w[r]) for r in range(4)]
                split.append(w)
            for ry in range(4):
                for rx in range(4):
                    weight_ref[l, ry * 4 + rx] = split[0][rx] * split[1][ry]
            s = jnp.tanh(displace_ref[2, l, h : h + 8, :])
            layers.append([0.5 * s * (s - 1.0), 1.0 - s * s, 0.5 * s * (s + 1.0)])

        def one_tracer(t, carry):
            totals = [None] * n_level
            for e in range(n_ext):
                at = pl.multiple_of((t * n_ext + e) * nblocks + h, 8)
                taken = []
                for ry in range(4):
                    values = patch_ref[pl.ds(at, 8), ry * 128 : (ry + 1) * 128]
                    for rx in range(4):
                        taken.append(take_lanes(values, index[ry][rx]))
                for l in range(n_level):
                    d = e - l
                    if 0 <= d <= 2:
                        acc = weight_ref[l, 0] * taken[0]
                        for kind in range(1, 16):
                            acc = acc + weight_ref[l, kind] * taken[kind]
                        acc = layers[l][d] * acc
                        totals[l] = acc if totals[l] is None else totals[l] + acc
            for l in range(n_level):
                out_ref[t, l, h : h + 8, :] = totals[l].astype(jnp.bfloat16)
            return carry

        lax.fori_loop(0, n_tracer, one_tracer, 0)


def body(tracers, wind_field, regions, stencil_base, far_start):
    n_tracer, n_level, nblocks, cells = tracers.shape
    own_band = lax.axis_index("tile")
    level_pos = lax.axis_index("lev")
    place = jnp.stack([own_band, level_pos, jnp.int32(lax.axis_size("lev"))]).astype(jnp.int32)
    packet = jnp.concatenate([wind_field, tracers], axis=0)
    lo1 = shifted(packet, "tile", 1)
    hi1 = shifted(packet, "tile", -1)
    lo2 = shifted(packet, "tile", 2)
    hi2 = shifted(packet, "tile", -2)
    bands = (lo2, lo1, packet, hi1, hi2)
    smem = pl.BlockSpec(memory_space=pltpu.SMEM)
    vmem = pl.BlockSpec(memory_space=pltpu.VMEM)
    params = pltpu.CompilerParams(vmem_limit_bytes=40 * 1024 * 1024)
    tops = jnp.concatenate([b[3:, n_level - 1] for b in bands], axis=1)
    bottoms = jnp.concatenate([b[3:, 0] for b in bands], axis=1)
    below = shifted(tops, "lev", 1)
    above = shifted(bottoms, "lev", -1)
    displacement = pl.pallas_call(
        wind_kernel,
        name="wind",
        out_shape=jax.ShapeDtypeStruct((3, n_level, nblocks, cells), jnp.float32),
        in_specs=[smem, smem] + [vmem] * 7,
        out_specs=vmem,
        scratch_shapes=[
            pltpu.VMEM((ITERS * 3 * n_level * nblocks, POINTS), jnp.bfloat16),
            pltpu.VMEM((ITERS * 3 * n_level * nblocks, POINTS), jnp.float32),
        ],
        compiler_params=params,
    )(place, far_start, regions, stencil_base, *bands)
    rows = n_tracer * (n_level + 2) * nblocks
    tracers_new = pl.pallas_call(
        tracer_kernel,
        name="tracer",
        out_shape=jax.ShapeDtypeStruct(tracers.shape, jnp.bfloat16),
        in_specs=[smem, smem] + [vmem] * 10,
        out_specs=vmem,
        scratch_shapes=[
            pltpu.VMEM((rows, POINTS), jnp.bfloat16),
            pltpu.VMEM((rows, POINTS), jnp.float32),
            pltpu.VMEM((n_level, 16, 8, 128), jnp.float32),
        ],
        compiler_params=params,
    )(place, far_start, regions, stencil_base, displacement, below, above, *bands)
    return (tracers_new, displacement)


def solution(mesh):
    return jax.shard_map(
        body,
        mesh=mesh,
        in_specs=(
            P(None, "lev", "tile", None),
            P(None, "lev", "tile", None),
            P(None, "tile", None),
            P(None, None, "tile", None),
            P(),
        ),
        out_specs=(P(None, "lev", "tile", None), P(None, "lev", "tile", None)),
        check_vma=False,
    )
```

profile of v0, /device:TPU:230, one launch (start us, length us, event | category | flops | bytes accessed | tf_op | source)
XLA Modules:
  0.0 50.6 jit_solution(2831420240871928751)
XLA Ops:
  0.6 0.8 %constant_dynamic-update-slice_fusion.1 = bf16[11,4,16,128]{3,2,1,0:T(8,128)(2,1)S(1)} fusion(bf16[3,4,16,128]{3,2,1,0:T(8,128)(2,1)} %param.6), kind=kLoop, calls=%fused_computation.19 | loop fusion | bytes 98304
  1.4 0.9 %constant_dynamic-update-slice_fusion.mid = bf16[11,4,16,128]{3,2,1,0:T(8,128)(2,1)S(1)} fusion(bf16[11,4,16,128]{3,2,1,0:T(8,128)(2,1)S(1)} %constant_dynamic-update-slice_fusion.1, bf16[8,4,16,128]{3,2,1,0:T(8,128)(2,1)} %param.5), kind=kLoop, calls=%fused_computation.18 | loop fusion | bytes 262144 | tf_op jit(solution)/shard_map/concatenate | solution.py:253
  2.4 0.0 copy-start.2
  2.4 5.5 %collective-permute-start = (bf16[11,4,16,128]{3,2,0,1:T(8,128)(2,1)S(1)}, bf16[11,4,16,128]{3,2,0,1:T(8,128)(2,1)S(1)}, u32[]{:S(2)}, u32[]{:S(2)}) collective-permute-start(bf16[11,4,16,128]{3,2,0,1:T(8,128)(2,1)S(1)} %copy.25), channel_id=1, source_target_pairs={{0,16},{8,24},{16,32},{24,40},{32,48},{40,56},{48,64},{56,72},{64,... | collective-permute-start | bytes 540680 | tf_op jit(solution)/shard_map/ppermute | solution.py:20
  7.9 1.9 %collective-permute-start.1 = (bf16[11,4,16,128]{3,2,0,1:T(8,128)(2,1)S(1)}, bf16[11,4,16,128]{3,2,0,1:T(8,128)(2,1)S(1)}, u32[]{:S(2)}, u32[]{:S(2)}) collective-permute-start(bf16[11,4,16,128]{3,2,0,1:T(8,128)(2,1)S(1)} %copy.25), channel_id=1, source_target_pairs={{0,8},{8,16},{16,24},{24,32},{32,40},{40,48},{48,56},{56,64},{64,7... | collective-permute-start | bytes 540680 | tf_op jit(solution)/shard_map/ppermute | solution.py:20
  9.9 3.6 %collective-permute-start.2 = (bf16[11,4,16,128]{3,2,0,1:T(8,128)(2,1)S(1)}, bf16[11,4,16,128]{3,2,0,1:T(8,128)(2,1)S(1)}, u32[]{:S(2)}, u32[]{:S(2)}) collective-permute-start(bf16[11,4,16,128]{3,2,0,1:T(8,128)(2,1)S(1)} %copy.25), channel_id=1, source_target_pairs={{8,0},{16,8},{24,16},{32,24},{40,32},{48,40},{56,48},{64,56},{72,6... | collective-permute-start | bytes 540680 | tf_op jit(solution)/shard_map/ppermute | solution.py:20
  13.5 1.9 %collective-permute-start.3 = (bf16[11,4,16,128]{3,2,1,0:T(8,128)(2,1)S(1)}, bf16[11,4,16,128]{3,2,1,0:T(8,128)(2,1)S(1)}, u32[]{:S(2)}, u32[]{:S(2)}) collective-permute-start(bf16[11,4,16,128]{3,2,1,0:T(8,128)(2,1)S(1)} %constant_dynamic-update-slice_fusion.mid), channel_id=1, source_target_pairs={{16,0},{24,8},{32,16},{40,24},{48,32},{56,40},{64,48},{72,56},{80,... | collective-permute-start | bytes 540680 | tf_op jit(solution)/shard_map/ppermute | solution.py:20
  15.4 0.0 collective-permute-done
  15.5 0.0 collective-permute-done.1
  15.5 0.0 copy-done.2
  15.5 1.5 %collective-permute-done.2 = bf16[11,4,16,128]{3,2,0,1:T(8,128)(2,1)S(1)} collective-permute-done((bf16[11,4,16,128]{3,2,0,1:T(8,128)(2,1)S(1)}, bf16[11,4,16,128]{3,2,0,1:T(8,128)(2,1)S(1)}, u32[]{:S(2)}, u32[]{:S(2)}) %collective-permute-start.2) | collective-permute-done | bytes 180256 | tf_op jit(solution)/shard_map/ppermute | solution.py:20
  17.0 8.6 %collective-permute-done.3.hi2 = bf16[11,4,16,128]{3,2,1,0:T(8,128)(2,1)S(1)} collective-permute-done((bf16[11,4,16,128]{3,2,1,0:T(8,128)(2,1)S(1)}, bf16[11,4,16,128]{3,2,1,0:T(8,128)(2,1)S(1)}, u32[]{:S(2)}, u32[]{:S(2)}) %collective-permute-start.3) | collective-permute-done | bytes 180256 | tf_op jit(solution)/shard_map/ppermute | solution.py:20
  25.6 2.6 %collective-permute-start.4 = (bf16[8,80,128]{2,1,0:T(8,128)(2,1)S(1)}, bf16[8,80,128]{2,1,0:T(8,128)(2,1)S(1)}, u32[]{:S(2)}, u32[]{:S(2)}) collective-permute-start(bf16[8,80,128]{2,1,0:T(8,128)(2,1)S(1)} %get-tuple-element.3), channel_id=1, source_target_pairs={{0,1},{1,2},{2,3},{3,4},{4,5},{5,6},{6,7},{8,9},{9,10},{10,11},{11... | collective-permute-start | bytes 491528 | tf_op jit(solution)/shard_map/ppermute | solution.py:20
  28.2 4.5 %collective-permute-start.5 = (bf16[8,80,128]{2,1,0:T(8,128)(2,1)S(1)}, bf16[8,80,128]{2,1,0:T(8,128)(2,1)S(1)}, u32[]{:S(2)}, u32[]{:S(2)}) collective-permute-start(bf16[8,80,128]{2,1,0:T(8,128)(2,1)S(1)} %get-tuple-element.2), channel_id=1, source_target_pairs={{1,0},{2,1},{3,2},{4,3},{5,4},{6,5},{7,6},{9,8},{10,9},{11,10},{12... | collective-permute-start | bytes 491528 | tf_op jit(solution)/shard_map/ppermute | solution.py:20
  32.7 0.0 copy-start.3
  32.7 0.7 %copy-done.3 = s32[4,64,2]{1,2,0:T(2,128)S(1)} copy-done((s32[4,64,2]{1,2,0:T(2,128)S(1)}, s32[4,64,2]{1,2,0:T(2,128)}, u32[]{:S(2)}) %copy-start.3) | copy-done | bytes 2072
  33.4 0.0 copy-start.4
  33.4 0.1 copy.19.far_ref
  33.5 0.6 %copy-done.4 = s32[4,16,2]{1,2,0:T(2,128)S(1)} copy-done((s32[4,16,2]{1,2,0:T(2,128)S(1)}, s32[4,16,2]{1,2,0:T(2,128)}, u32[]{:S(2)}) %copy-start.4) | copy-done | bytes 536
  34.1 0.1 copy.20.regions_ref
  34.2 0.1 pad_add_fusion.own_ref
  34.3 0.0 copy-start.1
  34.3 0.8 %copy-done.1 = s32[4,2,16,128]{3,2,1,0:T(8,128)S(1)} copy-done((s32[4,2,16,128]{3,2,1,0:T(8,128)S(1)}, s32[4,2,16,128]{3,2,1,0:T(8,128)}, u32[]{:S(2)}) %copy-start.1) | copy-done | bytes 65560
  35.2 4.8 %wind.1.displace_ref = f32[3,4,16,128]{3,2,1,0:T(8,128)} custom-call(s32[3]{0:T(128)S(1)} %pad_add_fusion.own_ref, s32[4,64,2]{2,1,0:T(8,128)S(1)} %copy.19.far_ref, s32[4,16,2]{2,1,0:T(8,128)S(1)} %copy.20.regions_ref, s32[4,2,16,128]{3,2,1,0:T(8,128)S(1)} %copy-done.1, bf16[11,4,16,128]{3,2,1,0:T(8,128)(2,1)S(1)} %copy.12.lo2, ...), custom_call_target="tpu_custom_call" | custom-call | tf_op jit(solution)/shard_map/wind/pallas_call | solution.py:266
  39.9 0.0 collective-permute-done.4.below_ref
  39.9 0.0 collective-permute-done.5.above_ref
  39.9 0.0 copy-start
  39.9 0.9 %copy-done = f32[3,4,16,128]{3,2,1,0:T(8,128)S(1)} copy-done((f32[3,4,16,128]{3,2,1,0:T(8,128)S(1)}, f32[3,4,16,128]{3,2,1,0:T(8,128)}, u32[]{:S(2)}) %copy-start) | copy-done | bytes 98328
  40.8 9.8 %tracer.1 = bf16[8,4,16,128]{3,2,1,0:T(8,128)(2,1)} custom-call(s32[3]{0:T(128)S(1)} %pad_add_fusion.own_ref, s32[4,64,2]{2,1,0:T(8,128)S(1)} %copy.19.far_ref, s32[4,16,2]{2,1,0:T(8,128)S(1)} %copy.20.regions_ref, s32[4,2,16,128]{3,2,1,0:T(8,128)S(1)} %copy-done.1, f32[3,4,16,128]{3,2,1,0:T(8,128)S(1)} %copy-done, ...), custom_call_target="tpu_custom_call" | custom-call | tf_op jit(solution)/shard_map/tracer/pallas_call | solution.py:279
  (9 shorter events, 0.1 us)
Async XLA Ops:
  2.4 13.1 %copy-start.2 = (bf16[8,4,16,128]{3,2,1,0:T(8,128)(2,1)S(1)}, bf16[8,4,16,128]{3,2,1,0:T(8,128)(2,1)}, u32[]{:S(2)}) copy-start(bf16[8,4,16,128]{3,2,1,0:T(8,128)(2,1)} %param.5) | copy-start | bytes 393220
  2.4 13.1 %collective-permute-start = (bf16[11,4,16,128]{3,2,0,1:T(8,128)(2,1)S(1)}, bf16[11,4,16,128]{3,2,0,1:T(8,128)(2,1)S(1)}, u32[]{:S(2)}, u32[]{:S(2)}) collective-permute-start(bf16[11,4,16,128]{3,2,0,1:T(8,128)(2,1)S(1)} %copy.25), channel_id=1, source_target_pairs={{0,16},{8,24},{16,32},{24,40},{32,48},{40,56},{48,64},{56,72},{64,... | collective-permute-start | bytes 540680 | tf_op jit(solution)/shard_map/ppermute | solution.py:20
  7.9 7.5 %collective-permute-start.1 = (bf16[11,4,16,128]{3,2,0,1:T(8,128)(2,1)S(1)}, bf16[11,4,16,128]{3,2,0,1:T(8,128)(2,1)S(1)}, u32[]{:S(2)}, u32[]{:S(2)}) collective-permute-start(bf16[11,4,16,128]{3,2,0,1:T(8,128)(2,1)S(1)} %copy.25), channel_id=1, source_target_pairs={{0,8},{8,16},{16,24},{24,32},{32,40},{40,48},{48,56},{56,64},{64,7... | collective-permute-start | bytes 540680 | tf_op jit(solution)/shard_map/ppermute | solution.py:20
  9.9 7.2 %collective-permute-start.2 = (bf16[11,4,16,128]{3,2,0,1:T(8,128)(2,1)S(1)}, bf16[11,4,16,128]{3,2,0,1:T(8,128)(2,1)S(1)}, u32[]{:S(2)}, u32[]{:S(2)}) collective-permute-start(bf16[11,4,16,128]{3,2,0,1:T(8,128)(2,1)S(1)} %copy.25), channel_id=1, source_target_pairs={{8,0},{16,8},{24,16},{32,24},{40,32},{48,40},{56,48},{64,56},{72,6... | collective-permute-start | bytes 540680 | tf_op jit(solution)/shard_map/ppermute | solution.py:20
  13.5 12.1 %collective-permute-start.3 = (bf16[11,4,16,128]{3,2,1,0:T(8,128)(2,1)S(1)}, bf16[11,4,16,128]{3,2,1,0:T(8,128)(2,1)S(1)}, u32[]{:S(2)}, u32[]{:S(2)}) collective-permute-start(bf16[11,4,16,128]{3,2,1,0:T(8,128)(2,1)S(1)} %constant_dynamic-update-slice_fusion.mid), channel_id=1, source_target_pairs={{16,0},{24,8},{32,16},{40,24},{48,32},{56,40},{64,48},{72,56},{80,... | collective-permute-start | bytes 540680 | tf_op jit(solution)/shard_map/ppermute | solution.py:20
  25.6 14.3 %collective-permute-start.4 = (bf16[8,80,128]{2,1,0:T(8,128)(2,1)S(1)}, bf16[8,80,128]{2,1,0:T(8,128)(2,1)S(1)}, u32[]{:S(2)}, u32[]{:S(2)}) collective-permute-start(bf16[8,80,128]{2,1,0:T(8,128)(2,1)S(1)} %get-tuple-element.3), channel_id=1, source_target_pairs={{0,1},{1,2},{2,3},{3,4},{4,5},{5,6},{6,7},{8,9},{9,10},{10,11},{11... | collective-permute-start | bytes 491528 | tf_op jit(solution)/shard_map/ppermute | solution.py:20
  28.2 11.7 %collective-permute-start.5 = (bf16[8,80,128]{2,1,0:T(8,128)(2,1)S(1)}, bf16[8,80,128]{2,1,0:T(8,128)(2,1)S(1)}, u32[]{:S(2)}, u32[]{:S(2)}) collective-permute-start(bf16[8,80,128]{2,1,0:T(8,128)(2,1)S(1)} %get-tuple-element.2), channel_id=1, source_target_pairs={{1,0},{2,1},{3,2},{4,3},{5,4},{6,5},{7,6},{9,8},{10,9},{11,10},{12... | collective-permute-start | bytes 491528 | tf_op jit(solution)/shard_map/ppermute | solution.py:20
  32.7 0.7 %copy-start.3 = (s32[4,64,2]{1,2,0:T(2,128)S(1)}, s32[4,64,2]{1,2,0:T(2,128)}, u32[]{:S(2)}) copy-start(s32[4,64,2]{1,2,0:T(2,128)} %param.9) | copy-start | bytes 6148
  33.4 0.7 %copy-start.4 = (s32[4,16,2]{1,2,0:T(2,128)S(1)}, s32[4,16,2]{1,2,0:T(2,128)}, u32[]{:S(2)}) copy-start(s32[4,16,2]{1,2,0:T(2,128)} %param.7) | copy-start | bytes 1540
  34.3 0.8 %copy-start.1 = (s32[4,2,16,128]{3,2,1,0:T(8,128)S(1)}, s32[4,2,16,128]{3,2,1,0:T(8,128)}, u32[]{:S(2)}) copy-start(s32[4,2,16,128]{3,2,1,0:T(8,128)} %base_ref.3) | copy-start | bytes 196612
  39.9 0.9 %copy-start = (f32[3,4,16,128]{3,2,1,0:T(8,128)S(1)}, f32[3,4,16,128]{3,2,1,0:T(8,128)}, u32[]{:S(2)}) copy-start(f32[3,4,16,128]{3,2,1,0:T(8,128)} %wind.1.displace_ref) | copy-start | bytes 294916
where the time goes:
time: 51.1 us; the launch traced here: 50.6 us
  starting transfers between devices  20.1 us (39%)
  Pallas kernels  14.6 us (29%)
  waiting for transfers between devices  10.1 us (20%)
  local copies, waits for them, and re-layouts  5.01 us (10%)
  between operations  0.8 us (2%)
    ppermute x6, starting transfers between devices, shifted(): return lax.ppermute(shard, axis, pairs)  20.1 us
    ppermute x6, waiting for transfers between devices, shifted(): return lax.ppermute(shard, axis, pairs)  10.1 us
    pallas_call x1, Pallas kernels, body(): pl.pallas_call(tracer_kernel, name='tracer', out_shape=jax.ShapeDtypeStru...  9.82 us
    pallas_call x1, Pallas kernels, body(): pl.pallas_call(wind_kernel, name='wind', out_shape=jax.ShapeDtypeStruct((...  4.77 us
    unnamed x17, local copies, waits for them, and re-layouts  4.02 us
  transfers between devices with their start and end apart: 6, of which 2 were waited for; matrix products, arithmetic and copies ran while one was open for 1% of the time, Pallas kernels for 9%

commit v1 on v0

v1 whole, which is shorter than its diff:
```python
import jax
import jax.numpy as jnp
from jax import lax
from jax.experimental import pallas as pl
from jax.experimental.pallas import tpu as pltpu
from jax.sharding import PartitionSpec as P

ITERS = 3
BW = 16
BH = 8
CELLS = BW * BH
QUADS = 4
POINTS = QUADS * CELLS
N_OFF = 5


def shifted(shard, axis, by):
    devices = lax.axis_size(axis)
    pairs = [(i, i + by) for i in range(devices) if 0 <= i + by < devices]
    return lax.ppermute(shard, axis, pairs)


def lagrange_cubic(position):
    return [
        -(position - 1.0) * (position - 2.0) * (position - 3.0) / 6.0,
        position * (position - 2.0) * (position - 3.0) / 2.0,
        -position * (position - 1.0) * (position - 3.0) / 2.0,
        position * (position - 1.0) * (position - 2.0) / 6.0,
    ]


def selectors(regions, own_band, start_low, start_high, nblocks):
    upper = regions[:, 0:1]
    left = regions[:, 1:2]
    lane = lax.broadcasted_iota(jnp.int32, (nblocks, N_OFF * nblocks), 1)
    rows = []
    for quad_y in (0, 1):
        for quad_x in (0, 1):
            offset = upper + (quad_y - own_band)
            col = (left + quad_x) & (nblocks - 1)
            run_low = (col - start_low) & (nblocks - 1)
            run_high = (col - start_high) & (nblocks - 1)
            run = jnp.where(offset == -2, run_low, jnp.where(offset == 2, run_high, 0))
            slot = jnp.where(run < nblocks // 2, (offset + 2) * nblocks + col, -1)
            rows.append(jnp.where(lane == slot, 1.0, 0.0).astype(jnp.bfloat16))
    return jnp.concatenate(rows, axis=0)


def class_order(log_step):
    step = 1 << log_step
    mask = step - 1
    source = lax.broadcasted_iota(jnp.int32, (POINTS, 128), 0)
    lane = lax.broadcasted_iota(jnp.int32, (POINTS, 128), 1)
    x = (source & (BW - 1)) + ((source >> 7) & 1) * BW
    y = ((source >> 4) & (BH - 1)) + (source >> 8) * BH
    kind = (y & mask) * step + (x & mask)
    place = (y >> log_step) * (2 * BW // step) + (x >> log_step)
    dest = kind * (POINTS // (step * step)) + place
    cols = [
        jnp.where(dest == lane + v * 128, 1.0, 0.0).astype(jnp.bfloat16) for v in range(QUADS)
    ]
    return jnp.concatenate(cols, axis=1)


def sort_rows(picked, nblocks, lanes_at):
    return jnp.concatenate(
        [
            picked[q * nblocks : (q + 1) * nblocks, lanes_at : lanes_at + CELLS]
            for q in range(QUADS)
        ],
        axis=1,
    )


LANES = lax.GatherDimensionNumbers(
    offset_dims=(),
    collapsed_slice_dims=(1,),
    start_index_map=(1,),
    operand_batching_dims=(0,),
    start_indices_batching_dims=(0,),
)


def take_lanes(values, index):
    picked = lax.gather(
        values,
        index[..., None],
        LANES,
        slice_sizes=(1, 1),
        mode=lax.GatherScatterMode.PROMISE_IN_BOUNDS,
    )
    return picked.astype(jnp.float32)


def wind_kernel(
    own_ref, regions_ref, base_ref, lo2, lo1, mid, hi1, hi2, out_ref, rows_ref, patch_ref
):
    n_comp, n_level, nblocks, _ = out_ref.shape
    own = own_ref[0]
    pick = jnp.concatenate(
        [
            selectors(regions_ref[k], own, own_ref[3 + 2 * k], own_ref[4 + 2 * k], nblocks)
            for k in range(ITERS)
        ],
        axis=0,
    )
    bands = (lo2, lo1, mid, hi1, hi2)
    fields = [(c, l) for c in range(n_comp) for l in range(n_level)]
    for i in range(0, len(fields), 2):
        pair = [
            jnp.concatenate([b[c, l] for b in bands], axis=0) for c, l in fields[i : i + 2]
        ]
        picked = jnp.dot(
            pick, jnp.concatenate(pair, axis=1), preferred_element_type=jnp.float32
        ).astype(jnp.bfloat16)
        for k in range(ITERS):
            part = picked[k * QUADS * nblocks : (k + 1) * QUADS * nblocks]
            for half in range(2):
                at = (k * len(fields) + i + half) * nblocks
                rows_ref[at : at + nblocks, :] = sort_rows(part, nblocks, half * CELLS)
    patch_ref[...] = jnp.dot(
        rows_ref[...], class_order(1), preferred_element_type=jnp.float32
    ).astype(jnp.bfloat16)
    displace = [[None] * n_comp for _ in range(n_level)]
    for k in range(ITERS):
        x0 = base_ref[k, 0] + 1
        y0 = base_ref[k, 1] + 1
        xs = [(x0 + 1) >> 1, x0 >> 1]
        ys = [((y0 + 1) >> 1) * BW, (y0 >> 1) * BW]
        index = [[(ys[ry] + xs[rx]).astype(jnp.int16) for rx in range(2)] for ry in range(2)]
        odd_x = (x0 & 1) == 1
        odd_y = (y0 & 1) == 1
        taken = {}
        for ry in range(2):
            for rx in range(2):
                kind = ry * 2 + rx
                for i in range(len(fields)):
                    at = (k * len(fields) + i) * nblocks
                    values = patch_ref[at : at + nblocks, kind * 128 : (kind + 1) * 128]
                    taken[i, kind] = take_lanes(values, index[ry][rx])
        for l in range(n_level):
            if k == 0:
                frac_x = jnp.full(x0.shape, 0.5, jnp.float32)
                frac_y = frac_x
            else:
                frac_x = 0.5 + 0.5 * jnp.tanh(displace[l][0])
                frac_y = 0.5 + 0.5 * jnp.tanh(displace[l][1])
            weight_x = [
                jnp.where(odd_x, frac_x, 1.0 - frac_x),
                jnp.where(odd_x, 1.0 - frac_x, frac_x),
            ]
            weight_y = [
                jnp.where(odd_y, frac_y, 1.0 - frac_y),
                jnp.where(odd_y, 1.0 - frac_y, frac_y),
            ]
            for c in range(n_comp):
                total = None
                for ry in range(2):
                    for rx in range(2):
                        term = weight_x[rx] * weight_y[ry] * taken[c * n_level + l, ry * 2 + rx]
                        total = term if total is None else total + term
                displace[l][c] = 0.5 * (mid[c, l].astype(jnp.float32) + total)
    for l in range(n_level):
        for c in range(n_comp):
            out_ref[c, l] = displace[l][c]


def tracer_kernel(
    own_ref,
    regions_ref,
    base_ref,
    displace_ref,
    below_ref,
    above_ref,
    lo2,
    lo1,
    mid,
    hi1,
    hi2,
    out_ref,
    rows_ref,
    patch_ref,
    weight_ref,
    layer_ref,
):
    n_tracer, n_level, nblocks, _ = out_ref.shape
    n_ext = n_level + 2
    first = lo2.shape[0] - n_tracer
    own = own_ref[0]
    at_bottom = own_ref[1] == 0
    at_top = own_ref[1] == own_ref[2] - 1
    k = ITERS
    pick = selectors(regions_ref[k], own, own_ref[3 + 2 * k], own_ref[4 + 2 * k], nblocks)
    bands = (lo2, lo1, mid, hi1, hi2)
    for t in range(n_tracer):
        levels = [
            jnp.concatenate([b[first + t, l] for b in bands], axis=0) for l in range(n_level)
        ]
        bottom = jnp.where(at_bottom, levels[0], below_ref[t])
        top = jnp.where(at_top, levels[-1], above_ref[t])
        levels = [bottom] + levels + [top]
        for e in range(0, n_ext, 2):
            picked = jnp.dot(
                pick,
                jnp.concatenate(levels[e : e + 2], axis=1),
                preferred_element_type=jnp.float32,
            ).astype(jnp.bfloat16)
            for half in range(2):
                at = (t * n_ext + e + half) * nblocks
                rows_ref[at : at + nblocks, :] = sort_rows(picked, nblocks, half * CELLS)
    patch_ref[...] = jnp.dot(
        rows_ref[...], class_order(2), preferred_element_type=jnp.float32
    ).astype(jnp.bfloat16)
    x0 = base_ref[k, 0]
    y0 = base_ref[k, 1]
    xs = [((x0 + ((r - x0) & 3)) >> 2) + r * 32 for r in range(4)]
    ys = [((y0 + ((r - y0) & 3)) >> 2) * 8 for r in range(4)]
    index = [(ys[ry] + xs[rx]).astype(jnp.int16) for ry in range(4) for rx in range(4)]
    for l in range(n_level):
        split = []
        for axis, start in ((0, x0), (1, y0)):
            w = lagrange_cubic(1.5 + 0.5 * jnp.tanh(displace_ref[axis, l]))
            bit0 = (start & 1) == 1
            bit1 = (start & 2) == 2
            w = [jnp.where(bit0, w[(r - 1) & 3], w[r]) for r in range(4)]
            w = [jnp.where(bit1, w[(r - 2) & 3], w[r]) for r in range(4)]
            split.append(w)
        for ry in range(4):
            for rx in range(4):
                weight_ref[ry * 4 + rx, l] = split[0][rx] * split[1][ry]
        s = jnp.tanh(displace_ref[2, l])
        layer_ref[l, 0] = 0.5 * s * (s - 1.0)
        layer_ref[l, 1] = 1.0 - s * s
        layer_ref[l, 2] = 0.5 * s * (s + 1.0)

    def one_tracer(t, carry):
        sums = {}
        for kind in range(16):
            at_lane = (kind // 4) * 128
            taken = []
            for e in range(n_ext):
                at = pl.multiple_of((t * n_ext + e) * nblocks, nblocks)
                values = patch_ref[pl.ds(at, nblocks), at_lane : at_lane + 128]
                taken.append(take_lanes(values, index[kind]))
            for l in range(n_level):
                weight = weight_ref[kind, l]
                for d in range(3):
                    term = weight * taken[l + d]
                    sums[l, d] = sums[l, d] + term if kind else term
        for l in range(n_level):
            total = layer_ref[l, 0] * sums[l, 0]
            total = total + layer_ref[l, 1] * sums[l, 1] + layer_ref[l, 2] * sums[l, 2]
            out_ref[t, l] = total.astype(jnp.bfloat16)
        return carry

    lax.fori_loop(0, n_tracer, one_tracer, 0)


def body(tracers, wind_field, regions, stencil_base, far_start):
    n_tracer, n_level, nblocks, cells = tracers.shape
    own_band = lax.axis_index("tile")
    level_pos = lax.axis_index("lev")
    n_bands = lax.axis_size("tile")
    starts = jnp.stack(
        [
            far_start[:, jnp.maximum(own_band - 2, 0), 0],
            far_start[:, jnp.minimum(own_band + 2, n_bands - 1), 1],
        ],
        axis=1,
    )
    ranks = jnp.stack([own_band, level_pos, jnp.int32(lax.axis_size("lev"))]).astype(jnp.int32)
    place = jnp.concatenate([ranks, starts.reshape(-1)])
    packet = jnp.concatenate([wind_field, tracers], axis=0)
    lo1 = shifted(packet, "tile", 1)
    hi1 = shifted(packet, "tile", -1)
    lo2 = shifted(packet, "tile", 2)
    hi2 = shifted(packet, "tile", -2)
    bands = (lo2, lo1, packet, hi1, hi2)
    smem = pl.BlockSpec(memory_space=pltpu.SMEM)
    vmem = pl.BlockSpec(memory_space=pltpu.VMEM)
    params = pltpu.CompilerParams(vmem_limit_bytes=40 * 1024 * 1024)
    tops = jnp.concatenate([b[3:, n_level - 1] for b in bands], axis=1)
    bottoms = jnp.concatenate([b[3:, 0] for b in bands], axis=1)
    below = shifted(tops, "lev", 1)
    above = shifted(bottoms, "lev", -1)
    displacement = pl.pallas_call(
        wind_kernel,
        name="wind",
        out_shape=jax.ShapeDtypeStruct((3, n_level, nblocks, cells), jnp.float32),
        in_specs=[smem] + [vmem] * 7,
        out_specs=vmem,
        scratch_shapes=[
            pltpu.VMEM((ITERS * 3 * n_level * nblocks, POINTS), jnp.bfloat16),
            pltpu.VMEM((ITERS * 3 * n_level * nblocks, POINTS), jnp.bfloat16),
        ],
        compiler_params=params,
    )(place, regions, stencil_base, *bands)
    rows = n_tracer * (n_level + 2) * nblocks
    tracers_new = pl.pallas_call(
        tracer_kernel,
        name="tracer",
        out_shape=jax.ShapeDtypeStruct(tracers.shape, jnp.bfloat16),
        in_specs=[smem] + [vmem] * 10,
        out_specs=vmem,
        scratch_shapes=[
            pltpu.VMEM((rows, POINTS), jnp.bfloat16),
            pltpu.VMEM((rows, POINTS), jnp.bfloat16),
            pltpu.VMEM((16, n_level, nblocks, cells), jnp.float32),
            pltpu.VMEM((n_level, 3, nblocks, cells), jnp.float32),
        ],
        compiler_params=params,
    )(place, regions, stencil_base, displacement, below, above, *bands)
    return (tracers_new, displacement)


def solution(mesh):
    return jax.shard_map(
        body,
        mesh=mesh,
        in_specs=(
            P(None, "lev", "tile", None),
            P(None, "lev", "tile", None),
            P(None, "tile", None),
            P(None, None, "tile", None),
            P(),
        ),
        out_specs=(P(None, "lev", "tile", None), P(None, "lev", "tile", None)),
        check_vma=False,
    )
```

time: 51.1 us -> 44.1 us (0.86)
  the two profiles are of different devices: /device:TPU:230 before, /device:TPU:222 now
where the time goes in v1:
time: 44.1 us; the launch traced here: 43.7 us
  starting transfers between devices  19.5 us (44%)
  waiting for transfers between devices  10.8 us (24%)
  Pallas kernels  6.34 us (14%)
  local copies, waits for them, and re-layouts  6.16 us (14%)
  between operations  0.81 us (2%)
    ppermute x6, starting transfers between devices, shifted(): return lax.ppermute(shard, axis, pairs)  19.5 us
    ppermute x6, waiting for transfers between devices, shifted(): return lax.ppermute(shard, axis, pairs)  10.8 us
    unnamed x16, local copies, waits for them, and re-layouts  4.69 us
    pallas_call x1, Pallas kernels, body(): pl.pallas_call(tracer_kernel, name='tracer', out_shape=jax.ShapeDtypeStru...  4.07 us
    pallas_call x1, Pallas kernels, body(): pl.pallas_call(wind_kernel, name='wind', out_shape=jax.ShapeDtypeStruct((...  2.27 us
    concatenate x2, local copies, waits for them, and re-layouts, body(): packet = jnp.concatenate([wind_field, tracers], axis=0)  0.94 us
  transfers between devices with their start and end apart: 6, of which 2 were waited for; matrix products, arithmetic and copies ran while one was open for 2% of the time, Pallas kernels for 5%

profile of v1, /device:TPU:222, one launch (start us, length us, event | category | flops | bytes accessed | tf_op | source)
XLA Modules:
  0.0 43.7 jit_solution(13520195823967885531)
XLA Ops:
  0.6 0.8 %constant_dynamic-update-slice_fusion.1 = bf16[11,4,16,128]{3,2,1,0:T(8,128)(2,1)S(1)} fusion(bf16[3,4,16,128]{3,2,1,0:T(8,128)(2,1)} %param.6), kind=kLoop, calls=%fused_computation.19 | loop fusion | bytes 98304
  1.4 0.9 %constant_dynamic-update-slice_fusion.mid = bf16[11,4,16,128]{3,2,1,0:T(8,128)(2,1)S(1)} fusion(bf16[11,4,16,128]{3,2,1,0:T(8,128)(2,1)S(1)} %constant_dynamic-update-slice_fusion.1, bf16[8,4,16,128]{3,2,1,0:T(8,128)(2,1)} %param.5), kind=kLoop, calls=%fused_computation.18 | loop fusion | bytes 262144 | tf_op jit(solution)/shard_map/concatenate | solution.py:273
  2.4 5.4 %collective-permute-start = (bf16[11,4,16,128]{3,2,0,1:T(8,128)(2,1)S(1)}, bf16[11,4,16,128]{3,2,0,1:T(8,128)(2,1)S(1)}, u32[]{:S(2)}, u32[]{:S(2)}) collective-permute-start(bf16[11,4,16,128]{3,2,0,1:T(8,128)(2,1)S(1)} %copy.41), channel_id=1, source_target_pairs={{0,16},{8,24},{16,32},{24,40},{32,48},{40,56},{48,64},{56,72},{64,... | collective-permute-start | bytes 540680 | tf_op jit(solution)/shard_map/ppermute | solution.py:20
  7.8 1.9 %collective-permute-start.1 = (bf16[11,4,16,128]{3,2,0,1:T(8,128)(2,1)S(1)}, bf16[11,4,16,128]{3,2,0,1:T(8,128)(2,1)S(1)}, u32[]{:S(2)}, u32[]{:S(2)}) collective-permute-start(bf16[11,4,16,128]{3,2,0,1:T(8,128)(2,1)S(1)} %copy.41), channel_id=1, source_target_pairs={{0,8},{8,16},{16,24},{24,32},{32,40},{40,48},{48,56},{56,64},{64,7... | collective-permute-start | bytes 540680 | tf_op jit(solution)/shard_map/ppermute | solution.py:20
  9.7 3.6 %collective-permute-start.2 = (bf16[11,4,16,128]{3,2,0,1:T(8,128)(2,1)S(1)}, bf16[11,4,16,128]{3,2,0,1:T(8,128)(2,1)S(1)}, u32[]{:S(2)}, u32[]{:S(2)}) collective-permute-start(bf16[11,4,16,128]{3,2,0,1:T(8,128)(2,1)S(1)} %copy.41), channel_id=1, source_target_pairs={{8,0},{16,8},{24,16},{32,24},{40,32},{48,40},{56,48},{64,56},{72,6... | collective-permute-start | bytes 540680 | tf_op jit(solution)/shard_map/ppermute | solution.py:20
  13.4 1.9 %collective-permute-start.3 = (bf16[11,4,16,128]{3,2,1,0:T(8,128)(2,1)S(1)}, bf16[11,4,16,128]{3,2,1,0:T(8,128)(2,1)S(1)}, u32[]{:S(2)}, u32[]{:S(2)}) collective-permute-start(bf16[11,4,16,128]{3,2,1,0:T(8,128)(2,1)S(1)} %constant_dynamic-update-slice_fusion.mid), channel_id=1, source_target_pairs={{16,0},{24,8},{32,16},{40,24},{48,32},{56,40},{64,48},{72,56},{80,... | collective-permute-start | bytes 540680 | tf_op jit(solution)/shard_map/ppermute | solution.py:20
  15.3 0.0 copy-start.4
  15.3 0.7 %copy-done.4 = s32[4,64,2]{1,2,0:T(2,128)S(1)} copy-done((s32[4,64,2]{1,2,0:T(2,128)S(1)}, s32[4,64,2]{1,2,0:T(2,128)}, u32[]{:S(2)}) %copy-start.4) | copy-done | bytes 2072
  16.0 0.3 dynamic-slice_reduce_fusion.1
  16.3 0.0 copy-start.2
  16.3 0.0 collective-permute-done
  16.3 0.0 collective-permute-done.1
  16.4 0.8 %copy-done.2 = bf16[8,4,16,128]{3,2,1,0:T(8,128)(2,1)S(1)} copy-done((bf16[8,4,16,128]{3,2,1,0:T(8,128)(2,1)S(1)}, bf16[8,4,16,128]{3,2,1,0:T(8,128)(2,1)}, u32[]{:S(2)}) %copy-start.2) | copy-done | bytes 131096
  17.2 0.0 collective-permute-done.2
  17.3 8.2 %collective-permute-done.3.hi2 = bf16[11,4,16,128]{3,2,1,0:T(8,128)(2,1)S(1)} collective-permute-done((bf16[11,4,16,128]{3,2,1,0:T(8,128)(2,1)S(1)}, bf16[11,4,16,128]{3,2,1,0:T(8,128)(2,1)S(1)}, u32[]{:S(2)}, u32[]{:S(2)}) %collective-permute-start.3) | collective-permute-done | bytes 180256 | tf_op jit(solution)/shard_map/ppermute | solution.py:20
  25.5 4.7 %collective-permute-start.4 = (bf16[8,80,128]{2,1,0:T(8,128)(2,1)S(1)}, bf16[8,80,128]{2,1,0:T(8,128)(2,1)S(1)}, u32[]{:S(2)}, u32[]{:S(2)}) collective-permute-start(bf16[8,80,128]{2,1,0:T(8,128)(2,1)S(1)} %get-tuple-element.5), channel_id=1, source_target_pairs={{0,1},{1,2},{2,3},{3,4},{4,5},{5,6},{6,7},{8,9},{9,10},{10,11},{11... | collective-permute-start | bytes 491528 | tf_op jit(solution)/shard_map/ppermute | solution.py:20
  30.2 1.9 %collective-permute-start.5 = (bf16[8,80,128]{2,1,0:T(8,128)(2,1)S(1)}, bf16[8,80,128]{2,1,0:T(8,128)(2,1)S(1)}, u32[]{:S(2)}, u32[]{:S(2)}) collective-permute-start(bf16[8,80,128]{2,1,0:T(8,128)(2,1)S(1)} %get-tuple-element.4), channel_id=1, source_target_pairs={{1,0},{2,1},{3,2},{4,3},{5,4},{6,5},{7,6},{9,8},{10,9},{11,10},{12... | collective-permute-start | bytes 491528 | tf_op jit(solution)/shard_map/ppermute | solution.py:20
  32.2 0.0 copy-start.3
  32.2 0.1 copy.24
  32.3 0.1 reshape.7
  32.3 0.5 %copy-done.3 = s32[4,16,2]{1,2,0:T(2,128)S(1)} copy-done((s32[4,16,2]{1,2,0:T(2,128)S(1)}, s32[4,16,2]{1,2,0:T(2,128)}, u32[]{:S(2)}) %copy-start.3) | copy-done | bytes 536
  32.8 0.1 copy.36.regions_ref
  32.9 0.1 pad_add_fusion.1.own_ref
  33.1 0.0 copy-start.1
  33.1 0.8 %copy-done.1 = s32[4,2,16,128]{3,2,1,0:T(8,128)S(1)} copy-done((s32[4,2,16,128]{3,2,1,0:T(8,128)S(1)}, s32[4,2,16,128]{3,2,1,0:T(8,128)}, u32[]{:S(2)}) %copy-start.1) | copy-done | bytes 65560
  33.9 2.3 %wind.1.displace_ref = f32[3,4,16,128]{3,2,1,0:T(8,128)} custom-call(s32[11]{0:T(128)S(1)} %pad_add_fusion.1.own_ref, s32[4,16,2]{2,1,0:T(8,128)S(1)} %copy.36.regions_ref, s32[4,2,16,128]{3,2,1,0:T(8,128)S(1)} %copy-done.1, bf16[11,4,16,128]{3,2,1,0:T(8,128)(2,1)S(1)} %copy.29.lo2, bf16[11,4,16,128]{3,2,1,0:T(8,128)(2,1)S(1)} %copy.30.lo1, ...), custom_call_target="tpu_custom_call" | custom-call | tf_op jit(solution)/shard_map/wind/pallas_call | solution.py:286
  36.2 0.0 collective-permute-done.4.below_ref
  36.2 2.5 %collective-permute-done.5.above_ref = bf16[8,80,128]{2,1,0:T(8,128)(2,1)S(1)} collective-permute-done((bf16[8,80,128]{2,1,0:T(8,128)(2,1)S(1)}, bf16[8,80,128]{2,1,0:T(8,128)(2,1)S(1)}, u32[]{:S(2)}, u32[]{:S(2)}) %collective-permute-start.5) | collective-permute-done | bytes 163872 | tf_op jit(solution)/shard_map/ppermute | solution.py:20
  38.7 0.0 copy-start
  38.7 0.9 %copy-done = f32[3,4,16,128]{3,2,1,0:T(8,128)S(1)} copy-done((f32[3,4,16,128]{3,2,1,0:T(8,128)S(1)}, f32[3,4,16,128]{3,2,1,0:T(8,128)}, u32[]{:S(2)}) %copy-start) | copy-done | bytes 98328
  39.6 4.1 %tracer.1 = bf16[8,4,16,128]{3,2,1,0:T(8,128)(2,1)} custom-call(s32[11]{0:T(128)S(1)} %pad_add_fusion.1.own_ref, s32[4,16,2]{2,1,0:T(8,128)S(1)} %copy.36.regions_ref, s32[4,2,16,128]{3,2,1,0:T(8,128)S(1)} %copy-done.1, f32[3,4,16,128]{3,2,1,0:T(8,128)S(1)} %copy-done, bf16[8,80,128]{2,1,0:T(8,128)(2,1)S(1)} %collective-permute-done.4.below_ref, ...), custom_call_target="tpu_custom_call" | custom-call | tf_op jit(solution)/shard_map/tracer/pallas_call | solution.py:299
  (10 shorter events, 0.1 us)
Async XLA Ops:
  2.4 13.9 %collective-permute-start = (bf16[11,4,16,128]{3,2,0,1:T(8,128)(2,1)S(1)}, bf16[11,4,16,128]{3,2,0,1:T(8,128)(2,1)S(1)}, u32[]{:S(2)}, u32[]{:S(2)}) collective-permute-start(bf16[11,4,16,128]{3,2,0,1:T(8,128)(2,1)S(1)} %copy.41), channel_id=1, source_target_pairs={{0,16},{8,24},{16,32},{24,40},{32,48},{40,56},{48,64},{56,72},{64,... | collective-permute-start | bytes 540680 | tf_op jit(solution)/shard_map/ppermute | solution.py:20
  7.8 8.5 %collective-permute-start.1 = (bf16[11,4,16,128]{3,2,0,1:T(8,128)(2,1)S(1)}, bf16[11,4,16,128]{3,2,0,1:T(8,128)(2,1)S(1)}, u32[]{:S(2)}, u32[]{:S(2)}) collective-permute-start(bf16[11,4,16,128]{3,2,0,1:T(8,128)(2,1)S(1)} %copy.41), channel_id=1, source_target_pairs={{0,8},{8,16},{16,24},{24,32},{32,40},{40,48},{48,56},{56,64},{64,7... | collective-permute-start | bytes 540680 | tf_op jit(solution)/shard_map/ppermute | solution.py:20
  9.7 7.5 %collective-permute-start.2 = (bf16[11,4,16,128]{3,2,0,1:T(8,128)(2,1)S(1)}, bf16[11,4,16,128]{3,2,0,1:T(8,128)(2,1)S(1)}, u32[]{:S(2)}, u32[]{:S(2)}) collective-permute-start(bf16[11,4,16,128]{3,2,0,1:T(8,128)(2,1)S(1)} %copy.41), channel_id=1, source_target_pairs={{8,0},{16,8},{24,16},{32,24},{40,32},{48,40},{56,48},{64,56},{72,6... | collective-permute-start | bytes 540680 | tf_op jit(solution)/shard_map/ppermute | solution.py:20
  13.4 12.1 %collective-permute-start.3 = (bf16[11,4,16,128]{3,2,1,0:T(8,128)(2,1)S(1)}, bf16[11,4,16,128]{3,2,1,0:T(8,128)(2,1)S(1)}, u32[]{:S(2)}, u32[]{:S(2)}) collective-permute-start(bf16[11,4,16,128]{3,2,1,0:T(8,128)(2,1)S(1)} %constant_dynamic-update-slice_fusion.mid), channel_id=1, source_target_pairs={{16,0},{24,8},{32,16},{40,24},{48,32},{56,40},{64,48},{72,56},{80,... | collective-permute-start | bytes 540680 | tf_op jit(solution)/shard_map/ppermute | solution.py:20
  15.3 0.7 %copy-start.4 = (s32[4,64,2]{1,2,0:T(2,128)S(1)}, s32[4,64,2]{1,2,0:T(2,128)}, u32[]{:S(2)}) copy-start(s32[4,64,2]{1,2,0:T(2,128)} %param.9) | copy-start | bytes 6148
  16.3 0.9 %copy-start.2 = (bf16[8,4,16,128]{3,2,1,0:T(8,128)(2,1)S(1)}, bf16[8,4,16,128]{3,2,1,0:T(8,128)(2,1)}, u32[]{:S(2)}) copy-start(bf16[8,4,16,128]{3,2,1,0:T(8,128)(2,1)} %param.5) | copy-start | bytes 393220
  25.5 10.7 %collective-permute-start.4 = (bf16[8,80,128]{2,1,0:T(8,128)(2,1)S(1)}, bf16[8,80,128]{2,1,0:T(8,128)(2,1)S(1)}, u32[]{:S(2)}, u32[]{:S(2)}) collective-permute-start(bf16[8,80,128]{2,1,0:T(8,128)(2,1)S(1)} %get-tuple-element.5), channel_id=1, source_target_pairs={{0,1},{1,2},{2,3},{3,4},{4,5},{5,6},{6,7},{8,9},{9,10},{10,11},{11... | collective-permute-start | bytes 491528 | tf_op jit(solution)/shard_map/ppermute | solution.py:20
  30.2 8.5 %collective-permute-start.5 = (bf16[8,80,128]{2,1,0:T(8,128)(2,1)S(1)}, bf16[8,80,128]{2,1,0:T(8,128)(2,1)S(1)}, u32[]{:S(2)}, u32[]{:S(2)}) collective-permute-start(bf16[8,80,128]{2,1,0:T(8,128)(2,1)S(1)} %get-tuple-element.4), channel_id=1, source_target_pairs={{1,0},{2,1},{3,2},{4,3},{5,4},{6,5},{7,6},{9,8},{10,9},{11,10},{12... | collective-permute-start | bytes 491528 | tf_op jit(solution)/shard_map/ppermute | solution.py:20
  32.2 0.7 %copy-start.3 = (s32[4,16,2]{1,2,0:T(2,128)S(1)}, s32[4,16,2]{1,2,0:T(2,128)}, u32[]{:S(2)}) copy-start(s32[4,16,2]{1,2,0:T(2,128)} %param.7) | copy-start | bytes 1540
  33.1 0.8 %copy-start.1 = (s32[4,2,16,128]{3,2,1,0:T(8,128)S(1)}, s32[4,2,16,128]{3,2,1,0:T(8,128)}, u32[]{:S(2)}) copy-start(s32[4,2,16,128]{3,2,1,0:T(8,128)} %base_ref.3) | copy-start | bytes 196612
  38.7 0.9 %copy-start = (f32[3,4,16,128]{3,2,1,0:T(8,128)S(1)}, f32[3,4,16,128]{3,2,1,0:T(8,128)}, u32[]{:S(2)}) copy-start(f32[3,4,16,128]{3,2,1,0:T(8,128)} %wind.1.displace_ref) | copy-start | bytes 294916

commit v2 on v1

v2 whole, which is shorter than its diff:
```python
import jax
import jax.numpy as jnp
from jax import lax
from jax.experimental import pallas as pl
from jax.experimental.pallas import tpu as pltpu
from jax.sharding import PartitionSpec as P

ITERS = 3
BW = 16
BH = 8
CELLS = BW * BH
QUADS = 4
POINTS = QUADS * CELLS
N_OFF = 5


def shifted(shard, axis, by):
    devices = lax.axis_size(axis)
    pairs = [(i, i + by) for i in range(devices) if 0 <= i + by < devices]
    return lax.ppermute(shard, axis, pairs)


def lagrange_cubic(position):
    return [
        -(position - 1.0) * (position - 2.0) * (position - 3.0) / 6.0,
        position * (position - 2.0) * (position - 3.0) / 2.0,
        -position * (position - 1.0) * (position - 3.0) / 2.0,
        position * (position - 1.0) * (position - 2.0) / 6.0,
    ]


def column(row, count):
    at = lax.broadcasted_iota(jnp.int32, (count, count), 0)
    lane = lax.broadcasted_iota(jnp.int32, (count, count), 1)
    return jnp.sum(jnp.where(at == lane, row, 0), axis=1, keepdims=True)


def selectors(regions, starts, own_band, nblocks):
    upper = column(regions[0:1], nblocks)
    left = column(regions[1:2], nblocks)
    mate = jnp.where((own_band & 1) == 0, 1, -1)
    lane = lax.broadcasted_iota(jnp.int32, (nblocks, N_OFF * nblocks), 1)
    rows = []
    for quad_y in (0, 1):
        for quad_x in (0, 1):
            offset = upper + (quad_y - own_band)
            col = (left + quad_x) & (nblocks - 1)
            run_low = (col - starts[0]) & (nblocks - 1)
            run_high = (col - starts[1]) & (nblocks - 1)
            run = jnp.where(offset == -2, run_low, jnp.where(offset == 2, run_high, 0))
            place = jnp.where(offset == mate, 1, jnp.where(offset == -mate, 3, offset + 2))
            slot = jnp.where(run < nblocks // 2, place * nblocks + col, -1)
            rows.append(jnp.where(lane == slot, 1.0, 0.0).astype(jnp.bfloat16))
    return jnp.concatenate(rows, axis=0)


def run_starts(far, own_band):
    n_bands = far.shape[1]
    lane = lax.broadcasted_iota(jnp.int32, (1, n_bands), 1)
    picked = []
    for side, band in ((0, own_band - 2), (1, own_band + 2)):
        band = jnp.clip(band, 0, n_bands - 1)
        picked.append(
            jnp.sum(jnp.where(lane == band, far[side : side + 1], 0), axis=1, keepdims=True)
        )
    return picked


def class_order(log_step):
    step = 1 << log_step
    mask = step - 1
    source = lax.broadcasted_iota(jnp.int32, (POINTS, 128), 0)
    lane = lax.broadcasted_iota(jnp.int32, (POINTS, 128), 1)
    x = (source & (BW - 1)) + ((source >> 7) & 1) * BW
    y = ((source >> 4) & (BH - 1)) + (source >> 8) * BH
    kind = (y & mask) * step + (x & mask)
    place = (y >> log_step) * (2 * BW // step) + (x >> log_step)
    dest = kind * (POINTS // (step * step)) + place
    cols = [
        jnp.where(dest == lane + v * 128, 1.0, 0.0).astype(jnp.bfloat16) for v in range(QUADS)
    ]
    return jnp.concatenate(cols, axis=1)


def sort_rows(picked, nblocks, lanes_at):
    return jnp.concatenate(
        [
            picked[q * nblocks : (q + 1) * nblocks, lanes_at : lanes_at + CELLS]
            for q in range(QUADS)
        ],
        axis=1,
    )


LANES = lax.GatherDimensionNumbers(
    offset_dims=(),
    collapsed_slice_dims=(1,),
    start_index_map=(1,),
    operand_batching_dims=(0,),
    start_indices_batching_dims=(0,),
)


def take_lanes(values, index):
    picked = lax.gather(
        values,
        index[..., None],
        LANES,
        slice_sizes=(1, 1),
        mode=lax.GatherScatterMode.PROMISE_IN_BOUNDS,
    )
    return picked.astype(jnp.float32)


def transport_kernel(
    far_ref,
    regions_ref,
    base_ref,
    mate,
    cross,
    hi2,
    lo2,
    mid,
    new_ref,
    displace_ref,
    wind_rows,
    wind_patch,
    rows_ref,
    patch_ref,
    weight_ref,
    layer_ref,
):
    n_tracer, n_level, nblocks, _ = new_ref.shape
    n_comp = displace_ref.shape[0]
    n_ext = n_level + 2
    own = lax.axis_index("tile")
    level_pos = lax.axis_index("lev")
    at_bottom = level_pos == 0
    at_top = level_pos == lax.axis_size("lev") - 1
    picks = [
        selectors(regions_ref[k], run_starts(far_ref[k], own), own, nblocks)
        for k in range(ITERS + 1)
    ]
    bands = (lo2, mate, mid, cross, hi2)

    def stacked(row):
        return jnp.concatenate([b[row] for b in bands], axis=0)

    n_field = n_comp * n_level
    pick = jnp.concatenate(picks[:ITERS], axis=0)
    for i in range(0, n_field, 2):
        picked = jnp.dot(
            pick,
            jnp.concatenate([stacked(i), stacked(i + 1)], axis=1),
            preferred_element_type=jnp.float32,
        ).astype(jnp.bfloat16)
        for k in range(ITERS):
            part = picked[k * QUADS * nblocks : (k + 1) * QUADS * nblocks]
            for half in range(2):
                at = (k * n_field + i + half) * nblocks
                wind_rows[at : at + nblocks, :] = sort_rows(part, nblocks, half * CELLS)
    wind_patch[...] = jnp.dot(
        wind_rows[...], class_order(1), preferred_element_type=jnp.float32
    ).astype(jnp.bfloat16)
    for t in range(n_tracer):
        levels = [stacked(n_field + t * n_level + l) for l in range(n_level)]
        below = stacked(n_field + n_tracer * n_level + t)
        above = stacked(n_field + n_tracer * (n_level + 1) + t)
        bottom = jnp.where(at_bottom, levels[0], below)
        top = jnp.where(at_top, levels[-1], above)
        levels = [bottom] + levels + [top]
        for e in range(0, n_ext, 2):
            picked = jnp.dot(
                picks[ITERS],
                jnp.concatenate(levels[e : e + 2], axis=1),
                preferred_element_type=jnp.float32,
            ).astype(jnp.bfloat16)
            for half in range(2):
                at = (t * n_ext + e + half) * nblocks
                rows_ref[at : at + nblocks, :] = sort_rows(picked, nblocks, half * CELLS)
    patch_ref[...] = jnp.dot(
        rows_ref[...], class_order(2), preferred_element_type=jnp.float32
    ).astype(jnp.bfloat16)
    displace = [[None] * n_comp for _ in range(n_level)]
    for k in range(ITERS):
        x0 = base_ref[k, 0] + 1
        y0 = base_ref[k, 1] + 1
        xs = [(x0 + 1) >> 1, x0 >> 1]
        ys = [((y0 + 1) >> 1) * BW, (y0 >> 1) * BW]
        index = [[(ys[ry] + xs[rx]).astype(jnp.int16) for rx in range(2)] for ry in range(2)]
        odd_x = (x0 & 1) == 1
        odd_y = (y0 & 1) == 1
        taken = {}
        for ry in range(2):
            for rx in range(2):
                kind = ry * 2 + rx
                for i in range(n_field):
                    at = (k * n_field + i) * nblocks
                    values = wind_patch[at : at + nblocks, kind * 128 : (kind + 1) * 128]
                    taken[i, kind] = take_lanes(values, index[ry][rx])
        for l in range(n_level):
            if k == 0:
                frac_x = jnp.full(x0.shape, 0.5, jnp.float32)
                frac_y = frac_x
            else:
                frac_x = 0.5 + 0.5 * jnp.tanh(displace[l][0])
                frac_y = 0.5 + 0.5 * jnp.tanh(displace[l][1])
            weight_x = [
                jnp.where(odd_x, frac_x, 1.0 - frac_x),
                jnp.where(odd_x, 1.0 - frac_x, frac_x),
            ]
            weight_y = [
                jnp.where(odd_y, frac_y, 1.0 - frac_y),
                jnp.where(odd_y, 1.0 - frac_y, frac_y),
            ]
            for c in range(n_comp):
                total = None
                for ry in range(2):
                    for rx in range(2):
                        term = weight_x[rx] * weight_y[ry] * taken[c * n_level + l, ry * 2 + rx]
                        total = term if total is None else total + term
                displace[l][c] = 0.5 * (mid[c * n_level + l].astype(jnp.float32) + total)
    for l in range(n_level):
        for c in range(n_comp):
            displace_ref[c, l] = displace[l][c]
    x0 = base_ref[ITERS, 0]
    y0 = base_ref[ITERS, 1]
    xs = [((x0 + ((r - x0) & 3)) >> 2) + r * 32 for r in range(4)]
    ys = [((y0 + ((r - y0) & 3)) >> 2) * 8 for r in range(4)]
    index = [(ys[ry] + xs[rx]).astype(jnp.int16) for ry in range(4) for rx in range(4)]
    for l in range(n_level):
        split = []
        for axis, start in ((0, x0), (1, y0)):
            w = lagrange_cubic(1.5 + 0.5 * jnp.tanh(displace[l][axis]))
            bit0 = (start & 1) == 1
            bit1 = (start & 2) == 2
            w = [jnp.where(bit0, w[(r - 1) & 3], w[r]) for r in range(4)]
            w = [jnp.where(bit1, w[(r - 2) & 3], w[r]) for r in range(4)]
            split.append(w)
        for ry in range(4):
            for rx in range(4):
                weight_ref[ry * 4 + rx, l] = split[0][rx] * split[1][ry]
        s = jnp.tanh(displace[l][2])
        layer_ref[l, 0] = 0.5 * s * (s - 1.0)
        layer_ref[l, 1] = 1.0 - s * s
        layer_ref[l, 2] = 0.5 * s * (s + 1.0)

    def one_tracer(t, carry):
        sums = {}
        for kind in range(16):
            at_lane = (kind // 4) * 128
            taken = []
            for e in range(n_ext):
                at = pl.multiple_of((t * n_ext + e) * nblocks, nblocks)
                values = patch_ref[pl.ds(at, nblocks), at_lane : at_lane + 128]
                taken.append(take_lanes(values, index[kind]))
            for l in range(n_level):
                weight = weight_ref[kind, l]
                for d in range(3):
                    term = weight * taken[l + d]
                    sums[l, d] = sums[l, d] + term if kind else term
        for l in range(n_level):
            total = layer_ref[l, 0] * sums[l, 0]
            total = total + layer_ref[l, 1] * sums[l, 1] + layer_ref[l, 2] * sums[l, 2]
            new_ref[t, l] = total.astype(jnp.bfloat16)
        return carry

    lax.fori_loop(0, n_tracer, one_tracer, 0)


def body(tracers, wind_field, regions, stencil_base, far_start):
    n_tracer, n_level, nblocks, cells = tracers.shape
    n_comp = wind_field.shape[0]
    n_bands = lax.axis_size("tile")
    below = shifted(tracers[:, n_level - 1], "lev", 1)
    above = shifted(tracers[:, 0], "lev", -1)
    packet = jnp.concatenate(
        [
            wind_field.reshape(-1, nblocks, cells),
            tracers.reshape(-1, nblocks, cells),
            below,
            above,
        ],
        axis=0,
    )
    lo2 = shifted(packet, "tile", 2)
    hi2 = shifted(packet, "tile", -2)
    cross = lax.ppermute(packet, "tile", [(i, ((i + 1) ^ 1) - 1) for i in range(1, n_bands - 1)])
    mate = lax.ppermute(packet, "tile", [(i, i ^ 1) for i in range(n_bands)])
    wind_rows = ITERS * n_comp * n_level * nblocks
    rows = n_tracer * (n_level + 2) * nblocks
    vmem = pl.BlockSpec(memory_space=pltpu.VMEM)
    return pl.pallas_call(
        transport_kernel,
        name="transport",
        out_shape=(
            jax.ShapeDtypeStruct(tracers.shape, jnp.bfloat16),
            jax.ShapeDtypeStruct(wind_field.shape, jnp.float32),
        ),
        in_specs=[vmem] * 8,
        out_specs=(vmem, vmem),
        scratch_shapes=[
            pltpu.VMEM((wind_rows, POINTS), jnp.bfloat16),
            pltpu.VMEM((wind_rows, POINTS), jnp.bfloat16),
            pltpu.VMEM((rows, POINTS), jnp.bfloat16),
            pltpu.VMEM((rows, POINTS), jnp.bfloat16),
            pltpu.VMEM((16, n_level, nblocks, cells), jnp.float32),
            pltpu.VMEM((n_level, 3, nblocks, cells), jnp.float32),
        ],
        compiler_params=pltpu.CompilerParams(vmem_limit_bytes=40 * 1024 * 1024),
    )(
        jnp.swapaxes(far_start, 1, 2),
        jnp.swapaxes(regions, 1, 2),
        stencil_base,
        mate,
        cross,
        hi2,
        lo2,
        packet,
    )


def solution(mesh):
    return jax.shard_map(
        body,
        mesh=mesh,
        in_specs=(
            P(None, "lev", "tile", None),
            P(None, "lev", "tile", None),
            P(None, "tile", None),
            P(None, None, "tile", None),
            P(),
        ),
        out_specs=(P(None, "lev", "tile", None), P(None, "lev", "tile", None)),
        check_vma=False,
    )
```

time: 44.1 us -> 38.6 us (0.88)
  the two profiles are of different devices: /device:TPU:222 before, /device:TPU:280 now
where the time goes in v2:
time: 38.6 us; the launch traced here: 38.3 us
  starting transfers between devices  19.6 us (51%)
  waiting for transfers between devices  12 us (31%)
  Pallas kernels  4.2 us (11%)
  other arithmetic  0.88 us (2%)
  local copies, waits for them, and re-layouts  0.85 us (2%)
  between operations  0.73 us (2%)
    ppermute x4, starting transfers between devices, shifted(): return lax.ppermute(shard, axis, pairs)  15.8 us
    ppermute x1, waiting for transfers between devices, body(): lax.ppermute(packet, 'tile', [(i, (i + 1 ^ 1) - 1) for i in range(1, n_ba...  6.96 us
    ppermute x4, waiting for transfers between devices, shifted(): return lax.ppermute(shard, axis, pairs)  5.09 us
    pallas_call x1, Pallas kernels, body(): pl.pallas_call(transport_kernel, name='transport', out_shape=(jax.ShapeDt...  4.2 us
    ppermute x1, starting transfers between devices, body(): lax.ppermute(packet, 'tile', [(i, (i + 1 ^ 1) - 1) for i in range(1, n_ba...  1.92 us
    ppermute x1, starting transfers between devices, body(): mate = lax.ppermute(packet, 'tile', [(i, i ^ 1) for i in range(n_bands)])  1.92 us
    concatenate x1, other arithmetic, body(): jnp.concatenate([wind_field.reshape(-1, nblocks, cells), tracers.reshape(...  0.88 us
    squeeze x1, local copies, waits for them, and re-layouts, body(): below = shifted(tracers[:, n_level - 1], 'lev', 1)  0.83 us
  transfers between devices with their start and end apart: 6, of which 2 were waited for; matrix products, arithmetic and copies ran while one was open for 0% of the time, Pallas kernels for 0%

profile of v2, /device:TPU:280, one launch (start us, length us, event | category | flops | bytes accessed | tf_op | source)
XLA Modules:
  0.0 38.3 jit_solution(8947020728230153516)
XLA Ops:
  0.6 0.0 copy-start.3
  0.6 0.8 %slice_bitcast_fusion.1 = (bf16[8,16,128]{2,1,0:T(8,128)(2,1)S(1)}, bf16[8,16,128]{2,1,0:T(8,128)(2,1)S(1)}) fusion(bf16[8,4,16,128]{3,2,1,0:T(8,128)(2,1)} %param.5), kind=kLoop, calls=%fused_computation.2 | loop fusion | bytes 131072 | tf_op jit(solution)/shard_map/squeeze | solution.py:275
  1.5 4.7 %collective-permute-start = (bf16[8,16,128]{2,1,0:T(8,128)(2,1)S(1)}, bf16[8,16,128]{2,1,0:T(8,128)(2,1)S(1)}, u32[]{:S(2)}, u32[]{:S(2)}) collective-permute-start(bf16[8,16,128]{2,1,0:T(8,128)(2,1)S(1)} %get-tuple-element.2), channel_id=1, source_target_pairs={{0,1},{1,2},{2,3},{3,4},{4,5},{5,6},{6,7},{8,9},{9,10},{10,11},{11... | collective-permute-start | bytes 98312 | tf_op jit(solution)/shard_map/ppermute | solution.py:20
  6.2 1.9 %collective-permute-start.1 = (bf16[8,16,128]{2,1,0:T(8,128)(2,1)S(1)}, bf16[8,16,128]{2,1,0:T(8,128)(2,1)S(1)}, u32[]{:S(2)}, u32[]{:S(2)}) collective-permute-start(bf16[8,16,128]{2,1,0:T(8,128)(2,1)S(1)} %get-tuple-element.3), channel_id=1, source_target_pairs={{1,0},{2,1},{3,2},{4,3},{5,4},{6,5},{7,6},{9,8},{10,9},{11,10},{12... | collective-permute-start | bytes 98312 | tf_op jit(solution)/shard_map/ppermute | solution.py:20
  8.1 0.0 collective-permute-done
  8.1 5.1 %collective-permute-done.1 = bf16[8,16,128]{2,1,0:T(8,128)(2,1)S(1)} collective-permute-done((bf16[8,16,128]{2,1,0:T(8,128)(2,1)S(1)}, bf16[8,16,128]{2,1,0:T(8,128)(2,1)S(1)}, u32[]{:S(2)}, u32[]{:S(2)}) %collective-permute-start.1) | collective-permute-done | bytes 32800 | tf_op jit(solution)/shard_map/ppermute | solution.py:20
  13.2 0.0 copy-done.3
  13.2 0.0 copy-start
  13.2 0.0 copy-start.1
  13.2 0.0 copy-start.2
  13.2 0.9 %pad_maximum_fusion.mid = bf16[60,16,128]{2,1,0:T(8,128)(2,1)S(1)} fusion(bf16[8,16,128]{2,1,0:T(8,128)(2,1)S(1)} %collective-permute-done.1, bf16[8,16,128]{2,1,0:T(8,128)(2,1)S(1)} %collective-permute-done, bf16[32,16,128]{2,1,0:T(8,128)(2,1)S(1)} %bitcast.14, bf16[12,16,128]{2,1,0:T(8,128)(2,1)} %bitcast.15), kind=kLoop, calls=%fused_computation | loop fusion | flops 368640 | bytes 491520 | tf_op jit(solution)/shard_map/concatenate | solution.py:277
  14.1 3.4 %collective-permute-start.5 = (bf16[60,16,128]{2,1,0:T(8,128)(2,1)S(1)}, bf16[60,16,128]{2,1,0:T(8,128)(2,1)S(1)}, u32[]{:S(2)}, u32[]{:S(2)}) collective-permute-start(bf16[60,16,128]{2,1,0:T(8,128)(2,1)S(1)} %pad_maximum_fusion.mid), channel_id=1, source_target_pairs={{0,16},{8,24},{16,32},{24,40},{32,48},{40,56},{48,64},{56,72},{64,... | collective-permute-start | bytes 737288 | tf_op jit(solution)/shard_map/ppermute | solution.py:20
  17.5 5.8 %collective-permute-start.4 = (bf16[60,16,128]{2,1,0:T(8,128)(2,1)S(1)}, bf16[60,16,128]{2,1,0:T(8,128)(2,1)S(1)}, u32[]{:S(2)}, u32[]{:S(2)}) collective-permute-start(bf16[60,16,128]{2,1,0:T(8,128)(2,1)S(1)} %pad_maximum_fusion.mid), channel_id=1, source_target_pairs={{16,0},{24,8},{32,16},{40,24},{48,32},{56,40},{64,48},{72,56},{80,... | collective-permute-start | bytes 737288 | tf_op jit(solution)/shard_map/ppermute | solution.py:20
  23.3 1.9 %collective-permute-start.3 = (bf16[60,16,128]{2,1,0:T(8,128)(2,1)S(1)}, bf16[60,16,128]{2,1,0:T(8,128)(2,1)S(1)}, u32[]{:S(2)}, u32[]{:S(2)}) collective-permute-start(bf16[60,16,128]{2,1,0:T(8,128)(2,1)S(1)} %pad_maximum_fusion.mid), channel_id=1, source_target_pairs={{8,16},{16,8},{24,32},{32,24},{40,48},{48,40},{56,64},{64,56},{72,... | collective-permute-start | bytes 737288 | tf_op jit(solution)/shard_map/ppermute | solution.py:288
  25.2 1.9 %collective-permute-start.2 = (bf16[60,16,128]{2,1,0:T(8,128)(2,1)S(1)}, bf16[60,16,128]{2,1,0:T(8,128)(2,1)S(1)}, u32[]{:S(2)}, u32[]{:S(2)}) collective-permute-start(bf16[60,16,128]{2,1,0:T(8,128)(2,1)S(1)} %pad_maximum_fusion.mid), channel_id=1, source_target_pairs={{0,8},{8,0},{16,24},{24,16},{32,40},{40,32},{48,56},{56,48},{64,72... | collective-permute-start | bytes 737288 | tf_op jit(solution)/shard_map/ppermute | solution.py:289
  27.1 0.0 collective-permute-done.5.lo2
  27.1 0.0 collective-permute-done.4.hi2
  27.1 7.0 %collective-permute-done.3.cross = bf16[60,16,128]{2,1,0:T(8,128)(2,1)S(1)} collective-permute-done((bf16[60,16,128]{2,1,0:T(8,128)(2,1)S(1)}, bf16[60,16,128]{2,1,0:T(8,128)(2,1)S(1)}, u32[]{:S(2)}, u32[]{:S(2)}) %collective-permute-start.3) | collective-permute-done | bytes 245792 | tf_op jit(solution)/shard_map/ppermute | solution.py:288
  34.1 0.0 collective-permute-done.2.mate
  34.1 0.0 copy-done
  34.1 0.0 copy-done.1
  34.1 0.0 copy-done.2
  34.1 4.2 %transport.1 = (bf16[8,4,16,128]{3,2,1,0:T(8,128)(2,1)}, f32[3,4,16,128]{3,2,1,0:T(8,128)}) custom-call(s32[4,2,64]{2,1,0:T(2,128)S(1)} %bitcast.12, s32[4,2,16]{2,1,0:T(2,128)S(1)} %bitcast.13, s32[4,2,16,128]{3,2,1,0:T(8,128)S(1)} %copy-done, bf16[60,16,128]{2,1,0:T(8,128)(2,1)S(1)} %collective-permute-done.2.mate, ...), custom_call_target="tpu_custom_call" | custom-call | tf_op jit(solution)/shard_map/transport/pallas_call | solution.py:293
Async XLA Ops:
  0.6 12.6 %copy-start.3 = (bf16[8,4,16,128]{3,2,1,0:T(8,128)(2,1)S(1)}, bf16[8,4,16,128]{3,2,1,0:T(8,128)(2,1)}, u32[]{:S(2)}) copy-start(bf16[8,4,16,128]{3,2,1,0:T(8,128)(2,1)} %param.5) | copy-start | bytes 393220
  1.5 6.6 %collective-permute-start = (bf16[8,16,128]{2,1,0:T(8,128)(2,1)S(1)}, bf16[8,16,128]{2,1,0:T(8,128)(2,1)S(1)}, u32[]{:S(2)}, u32[]{:S(2)}) collective-permute-start(bf16[8,16,128]{2,1,0:T(8,128)(2,1)S(1)} %get-tuple-element.2), channel_id=1, source_target_pairs={{0,1},{1,2},{2,3},{3,4},{4,5},{5,6},{6,7},{8,9},{9,10},{10,11},{11... | collective-permute-start | bytes 98312 | tf_op jit(solution)/shard_map/ppermute | solution.py:20
  6.2 7.0 %collective-permute-start.1 = (bf16[8,16,128]{2,1,0:T(8,128)(2,1)S(1)}, bf16[8,16,128]{2,1,0:T(8,128)(2,1)S(1)}, u32[]{:S(2)}, u32[]{:S(2)}) collective-permute-start(bf16[8,16,128]{2,1,0:T(8,128)(2,1)S(1)} %get-tuple-element.3), channel_id=1, source_target_pairs={{1,0},{2,1},{3,2},{4,3},{5,4},{6,5},{7,6},{9,8},{10,9},{11,10},{12... | collective-permute-start | bytes 98312 | tf_op jit(solution)/shard_map/ppermute | solution.py:20
  13.2 20.9 %copy-start = (s32[4,2,16,128]{3,2,1,0:T(8,128)S(1)}, s32[4,2,16,128]{3,2,1,0:T(8,128)}, u32[]{:S(2)}) copy-start(s32[4,2,16,128]{3,2,1,0:T(8,128)} %base_ref.1) | copy-start | bytes 196612
  13.2 20.9 %copy-start.1 = (s32[4,64,2]{1,2,0:T(2,128)S(1)}, s32[4,64,2]{1,2,0:T(2,128)}, u32[]{:S(2)}) copy-start(s32[4,64,2]{1,2,0:T(2,128)} %param.9) | copy-start | bytes 6148
  13.2 20.9 %copy-start.2 = (s32[4,16,2]{1,2,0:T(2,128)S(1)}, s32[4,16,2]{1,2,0:T(2,128)}, u32[]{:S(2)}) copy-start(s32[4,16,2]{1,2,0:T(2,128)} %param.7) | copy-start | bytes 1540
  14.1 13.0 %collective-permute-start.5 = (bf16[60,16,128]{2,1,0:T(8,128)(2,1)S(1)}, bf16[60,16,128]{2,1,0:T(8,128)(2,1)S(1)}, u32[]{:S(2)}, u32[]{:S(2)}) collective-permute-start(bf16[60,16,128]{2,1,0:T(8,128)(2,1)S(1)} %pad_maximum_fusion.mid), channel_id=1, source_target_pairs={{0,16},{8,24},{16,32},{24,40},{32,48},{40,56},{48,64},{56,72},{64,... | collective-permute-start | bytes 737288 | tf_op jit(solution)/shard_map/ppermute | solution.py:20
  17.5 9.6 %collective-permute-start.4 = (bf16[60,16,128]{2,1,0:T(8,128)(2,1)S(1)}, bf16[60,16,128]{2,1,0:T(8,128)(2,1)S(1)}, u32[]{:S(2)}, u32[]{:S(2)}) collective-permute-start(bf16[60,16,128]{2,1,0:T(8,128)(2,1)S(1)} %pad_maximum_fusion.mid), channel_id=1, source_target_pairs={{16,0},{24,8},{32,16},{40,24},{48,32},{56,40},{64,48},{72,56},{80,... | collective-permute-start | bytes 737288 | tf_op jit(solution)/shard_map/ppermute | solution.py:20
  23.3 10.8 %collective-permute-start.3 = (bf16[60,16,128]{2,1,0:T(8,128)(2,1)S(1)}, bf16[60,16,128]{2,1,0:T(8,128)(2,1)S(1)}, u32[]{:S(2)}, u32[]{:S(2)}) collective-permute-start(bf16[60,16,128]{2,1,0:T(8,128)(2,1)S(1)} %pad_maximum_fusion.mid), channel_id=1, source_target_pairs={{8,16},{16,8},{24,32},{32,24},{40,48},{48,40},{56,64},{64,56},{72,... | collective-permute-start | bytes 737288 | tf_op jit(solution)/shard_map/ppermute | solution.py:288
  25.2 8.9 %collective-permute-start.2 = (bf16[60,16,128]{2,1,0:T(8,128)(2,1)S(1)}, bf16[60,16,128]{2,1,0:T(8,128)(2,1)S(1)}, u32[]{:S(2)}, u32[]{:S(2)}) collective-permute-start(bf16[60,16,128]{2,1,0:T(8,128)(2,1)S(1)} %pad_maximum_fusion.mid), channel_id=1, source_target_pairs={{0,8},{8,0},{16,24},{24,16},{32,40},{40,32},{48,56},{56,48},{64,72... | collective-permute-start | bytes 737288 | tf_op jit(solution)/shard_map/ppermute | solution.py:289

commit v3 on v2

--- a/solution.py
+++ b/solution.py
@@ -14,9 +14,13 @@
 N_OFF = 5
 
 
-def shifted(shard, axis, by):
+def swapped(shard, axis, first, by):
     devices = lax.axis_size(axis)
-    pairs = [(i, i + by) for i in range(devices) if 0 <= i + by < devices]
+    pairs = []
+    for i in range(first, devices):
+        j = ((i - first) ^ by) + first
+        if j < devices:
+            pairs.append((i, j))
     return lax.ppermute(shard, axis, pairs)
 
 
@@ -39,6 +43,7 @@
     upper = column(regions[0:1], nblocks)
     left = column(regions[1:2], nblocks)
     mate = jnp.where((own_band & 1) == 0, 1, -1)
+    paired = jnp.where((own_band & 2) == 0, 2, -2)
     lane = lax.broadcasted_iota(jnp.int32, (nblocks, N_OFF * nblocks), 1)
     rows = []
     for quad_y in (0, 1):
@@ -48,7 +53,8 @@
             run_low = (col - starts[0]) & (nblocks - 1)
             run_high = (col - starts[1]) & (nblocks - 1)
             run = jnp.where(offset == -2, run_low, jnp.where(offset == 2, run_high, 0))
-            place = jnp.where(offset == mate, 1, jnp.where(offset == -mate, 3, offset + 2))
+            place = jnp.where(offset == mate, 1, jnp.where(offset == -mate, 3, 2))
+            place = jnp.where(offset == paired, 4, jnp.where(offset == -paired, 0, place))
             slot = jnp.where(run < nblocks // 2, place * nblocks + col, -1)
             rows.append(jnp.where(lane == slot, 1.0, 0.0).astype(jnp.bfloat16))
     return jnp.concatenate(rows, axis=0)
@@ -118,8 +124,8 @@
     base_ref,
     mate,
     cross,
-    hi2,
-    lo2,
+    even2,
+    odd2,
     mid,
     new_ref,
     displace_ref,
@@ -134,14 +140,11 @@
     n_comp = displace_ref.shape[0]
     n_ext = n_level + 2
     own = lax.axis_index("tile")
-    level_pos = lax.axis_index("lev")
-    at_bottom = level_pos == 0
-    at_top = level_pos == lax.axis_size("lev") - 1
     picks = [
         selectors(regions_ref[k], run_starts(far_ref[k], own), own, nblocks)
         for k in range(ITERS + 1)
     ]
-    bands = (lo2, mate, mid, cross, hi2)
+    bands = (odd2, mate, mid, cross, even2)
 
     def stacked(row):
         return jnp.concatenate([b[row] for b in bands], axis=0)
@@ -166,9 +169,7 @@
         levels = [stacked(n_field + t * n_level + l) for l in range(n_level)]
         below = stacked(n_field + n_tracer * n_level + t)
         above = stacked(n_field + n_tracer * (n_level + 1) + t)
-        bottom = jnp.where(at_bottom, levels[0], below)
-        top = jnp.where(at_top, levels[-1], above)
-        levels = [bottom] + levels + [top]
+        levels = [below] + levels + [above]
         for e in range(0, n_ext, 2):
             picked = jnp.dot(
                 picks[ITERS],
@@ -271,22 +272,26 @@
 def body(tracers, wind_field, regions, stencil_base, far_start):
     n_tracer, n_level, nblocks, cells = tracers.shape
     n_comp = wind_field.shape[0]
-    n_bands = lax.axis_size("tile")
-    below = shifted(tracers[:, n_level - 1], "lev", 1)
-    above = shifted(tracers[:, 0], "lev", -1)
+    level_pos = lax.axis_index("lev")
+    even = level_pos % 2 == 0
+    bottom, top = tracers[:, 0], tracers[:, n_level - 1]
+    got_odd = swapped(jnp.where(even, bottom, top), "lev", 1, 1)
+    got_even = swapped(jnp.where(even, top, bottom), "lev", 0, 1)
+    below = jnp.where(even, got_odd, got_even)
+    above = jnp.where(even, got_even, got_odd)
     packet = jnp.concatenate(
         [
             wind_field.reshape(-1, nblocks, cells),
             tracers.reshape(-1, nblocks, cells),
-            below,
-            above,
+            jnp.where(level_pos == 0, bottom, below),
+            jnp.where(level_pos == lax.axis_size("lev") - 1, top, above),
         ],
         axis=0,
     )
-    lo2 = shifted(packet, "tile", 2)
-    hi2 = shifted(packet, "tile", -2)
-    cross = lax.ppermute(packet, "tile", [(i, ((i + 1) ^ 1) - 1) for i in range(1, n_bands - 1)])
-    mate = lax.ppermute(packet, "tile", [(i, i ^ 1) for i in range(n_bands)])
+    odd2 = swapped(packet, "tile", 2, 2)
+    even2 = swapped(packet, "tile", 0, 2)
+    cross = swapped(packet, "tile", 1, 1)
+    mate = swapped(packet, "tile", 0, 1)
     wind_rows = ITERS * n_comp * n_level * nblocks
     rows = n_tracer * (n_level + 2) * nblocks
     vmem = pl.BlockSpec(memory_space=pltpu.VMEM)
@@ -314,8 +319,8 @@
         stencil_base,
         mate,
         cross,
-        hi2,
-        lo2,
+        even2,
+        odd2,
         packet,
     )
 

time: 38.6 us -> 34.2 us (0.89)
  waiting for transfers between devices: 12 us -> 9.85 us
  starting transfers between devices: 19.6 us -> 18.2 us
  local copies, waits for them, and re-layouts: 0.85 us -> 0.03 us
    ppermute x6, waiting for transfers between devices: 12 us -> 9.85 us  [swapped(): return lax.ppermute(shard, axis, pairs)]
    ppermute x6, starting transfers between devices: 19.6 us -> 18.2 us  [swapped(): return lax.ppermute(shard, axis, pairs)]
    concatenate x1, other arithmetic: 0.88 us -> 0.04 us  [body(): jnp.concatenate([wind_field.reshape(-1, nblocks, cells), tracers.reshape(...]
    select_n x0 -> x2, other arithmetic: none -> 0.83 us  [the longest x1 0.82 us: body(): got_odd = swapped(jnp.where(even, bottom, top), 'lev', 1, 1)]
    squeeze x1 -> x0, local copies, waits for them, and re-layouts: 0.83 us -> none  [body(): below = shifted(tracers[:, n_level - 1], 'lev', 1)]
  transfers between devices with their start and end apart: 6 -> 6, of which waited for: 2 -> 4; matrix products, arithmetic and copies ran while one was open for 0% -> 0% of each run, Pallas kernels for 0% -> 0%
where the time goes in v3:
time: 34.2 us; the launch traced here: 34 us
  starting transfers between devices  18.2 us (53%)
  waiting for transfers between devices  9.85 us (29%)
  Pallas kernels  4.2 us (12%)
  other arithmetic  0.87 us (3%)
  between operations  0.78 us (2%)
    ppermute x6, starting transfers between devices, swapped(): return lax.ppermute(shard, axis, pairs)  18.2 us
    ppermute x6, waiting for transfers between devices, swapped(): return lax.ppermute(shard, axis, pairs)  9.85 us
    pallas_call x1, Pallas kernels, body(): pl.pallas_call(transport_kernel, name='transport', out_shape=(jax.ShapeDt...  4.2 us
    select_n x1, other arithmetic, body(): got_odd = swapped(jnp.where(even, bottom, top), 'lev', 1, 1)  0.82 us
  transfers between devices with their start and end apart: 6, of which 4 were waited for; matrix products, arithmetic and copies ran while one was open for 0% of the time, Pallas kernels for 0%

profile of v3, /device:TPU:280, one launch (start us, length us, event | category | flops | bytes accessed | tf_op | source)
XLA Modules:
  0.0 34.0 jit_solution(437706348551352156)
XLA Ops:
  0.6 0.0 copy-start.3
  0.7 0.8 %bitcast_select_fusion.2 = (bf16[8,16,128]{2,1,0:T(8,128)(2,1)S(1)}, bf16[8,16,128]{2,1,0:T(8,128)(2,1)S(1)}) fusion(pred[]{:T(512)S(6)} %eq.12, bf16[8,4,16,128]{3,2,1,0:T(8,128)(2,1)} %param.5), kind=kLoop, calls=%fused_computation.3 | loop fusion | flops 32768 | bytes 131073 | tf_op jit(solution)/shard_map/jit(_where)/select_n | solution.py:278
  1.5 4.7 %collective-permute-start = (bf16[8,16,128]{2,1,0:T(8,128)(2,1)S(1)}, bf16[8,16,128]{2,1,0:T(8,128)(2,1)S(1)}, u32[]{:S(2)}, u32[]{:S(2)}) collective-permute-start(bf16[8,16,128]{2,1,0:T(8,128)(2,1)S(1)} %get-tuple-element.4), channel_id=1, source_target_pairs={{1,2},{2,1},{3,4},{4,3},{5,6},{6,5},{9,10},{10,9},{11,12},{12,11},... | collective-permute-start | bytes 98312 | tf_op jit(solution)/shard_map/ppermute | solution.py:24
  6.2 1.9 %collective-permute-start.1 = (bf16[8,16,128]{2,1,0:T(8,128)(2,1)S(1)}, bf16[8,16,128]{2,1,0:T(8,128)(2,1)S(1)}, u32[]{:S(2)}, u32[]{:S(2)}) collective-permute-start(bf16[8,16,128]{2,1,0:T(8,128)(2,1)S(1)} %get-tuple-element.5), channel_id=1, source_target_pairs={{0,1},{1,0},{2,3},{3,2},{4,5},{5,4},{6,7},{7,6},{8,9},{9,8},{10,11... | collective-permute-start | bytes 98312 | tf_op jit(solution)/shard_map/ppermute | solution.py:24
  8.1 0.0 copy-start.4
  8.1 0.4 %collective-permute-done = bf16[8,16,128]{2,1,0:T(8,128)(2,1)S(1)} collective-permute-done((bf16[8,16,128]{2,1,0:T(8,128)(2,1)S(1)}, bf16[8,16,128]{2,1,0:T(8,128)(2,1)S(1)}, u32[]{:S(2)}, u32[]{:S(2)}) %collective-permute-start) | collective-permute-done | bytes 32800 | tf_op jit(solution)/shard_map/ppermute | solution.py:24
  8.5 3.5 %collective-permute-done.1 = bf16[8,16,128]{2,1,0:T(8,128)(2,1)S(1)} collective-permute-done((bf16[8,16,128]{2,1,0:T(8,128)(2,1)S(1)}, bf16[8,16,128]{2,1,0:T(8,128)(2,1)S(1)}, u32[]{:S(2)}, u32[]{:S(2)}) %collective-permute-start.1) | collective-permute-done | bytes 32800 | tf_op jit(solution)/shard_map/ppermute | solution.py:24
  12.0 0.0 copy-done.3
  12.0 0.0 copy-done.4
  12.0 0.0 copy-start
  12.0 0.0 copy-start.1
  12.0 0.0 copy-start.2
  12.1 3.8 %collective-permute-start.5 = (bf16[60,16,128]{2,1,0:T(8,128)(2,1)S(1)}, bf16[60,16,128]{2,1,0:T(8,128)(2,1)S(1)}, u32[]{:S(2)}, u32[]{:S(2)}) collective-permute-start(bf16[60,16,128]{2,1,0:T(8,128)(2,1)S(1)} %pad_maximum_fusion.mid), channel_id=1, source_target_pairs={{16,32},{24,40},{32,16},{40,24},{48,64},{56,72},{64,48},{72,56},{8... | collective-permute-start | bytes 737288 | tf_op jit(solution)/shard_map/ppermute | solution.py:24
  15.9 3.0 %collective-permute-start.4 = (bf16[60,16,128]{2,1,0:T(8,128)(2,1)S(1)}, bf16[60,16,128]{2,1,0:T(8,128)(2,1)S(1)}, u32[]{:S(2)}, u32[]{:S(2)}) collective-permute-start(bf16[60,16,128]{2,1,0:T(8,128)(2,1)S(1)} %pad_maximum_fusion.mid), channel_id=1, source_target_pairs={{0,16},{8,24},{16,0},{24,8},{32,48},{40,56},{48,32},{56,40},{64,80... | collective-permute-start | bytes 737288 | tf_op jit(solution)/shard_map/ppermute | solution.py:24
  18.9 2.0 %collective-permute-start.3 = (bf16[60,16,128]{2,1,0:T(8,128)(2,1)S(1)}, bf16[60,16,128]{2,1,0:T(8,128)(2,1)S(1)}, u32[]{:S(2)}, u32[]{:S(2)}) collective-permute-start(bf16[60,16,128]{2,1,0:T(8,128)(2,1)S(1)} %pad_maximum_fusion.mid), channel_id=1, source_target_pairs={{8,16},{16,8},{24,32},{32,24},{40,48},{48,40},{56,64},{64,56},{72,... | collective-permute-start | bytes 737288 | tf_op jit(solution)/shard_map/ppermute | solution.py:24
  20.9 2.8 %collective-permute-start.2 = (bf16[60,16,128]{2,1,0:T(8,128)(2,1)S(1)}, bf16[60,16,128]{2,1,0:T(8,128)(2,1)S(1)}, u32[]{:S(2)}, u32[]{:S(2)}) collective-permute-start(bf16[60,16,128]{2,1,0:T(8,128)(2,1)S(1)} %pad_maximum_fusion.mid), channel_id=1, source_target_pairs={{0,8},{8,0},{16,24},{24,16},{32,40},{40,32},{48,56},{56,48},{64,72... | collective-permute-start | bytes 737288 | tf_op jit(solution)/shard_map/ppermute | solution.py:24
  23.8 0.0 collective-permute-done.5.odd2
  23.8 0.2 collective-permute-done.4.even2
  24.0 5.8 %collective-permute-done.3.cross = bf16[60,16,128]{2,1,0:T(8,128)(2,1)S(1)} collective-permute-done((bf16[60,16,128]{2,1,0:T(8,128)(2,1)S(1)}, bf16[60,16,128]{2,1,0:T(8,128)(2,1)S(1)}, u32[]{:S(2)}, u32[]{:S(2)}) %collective-permute-start.3) | collective-permute-done | bytes 245792 | tf_op jit(solution)/shard_map/ppermute | solution.py:24
  29.8 0.0 collective-permute-done.2.mate
  29.8 0.0 copy-done
  29.8 0.0 copy-done.1
  29.8 0.0 copy-done.2
  29.8 4.2 %transport.1 = (bf16[8,4,16,128]{3,2,1,0:T(8,128)(2,1)}, f32[3,4,16,128]{3,2,1,0:T(8,128)}) custom-call(s32[4,2,64]{2,1,0:T(2,128)S(1)} %bitcast.16, s32[4,2,16]{2,1,0:T(2,128)S(1)} %bitcast.17, s32[4,2,16,128]{3,2,1,0:T(8,128)S(1)} %copy-done, bf16[60,16,128]{2,1,0:T(8,128)(2,1)S(1)} %collective-permute-done.2.mate, ...), custom_call_target="tpu_custom_call" | custom-call | tf_op jit(solution)/shard_map/transport/pallas_call | solution.py:298
  (2 shorter events, 0.1 us)
Async XLA Ops:
  0.6 11.4 %copy-start.3 = (bf16[8,4,16,128]{3,2,1,0:T(8,128)(2,1)S(1)}, bf16[8,4,16,128]{3,2,1,0:T(8,128)(2,1)}, u32[]{:S(2)}) copy-start(bf16[8,4,16,128]{3,2,1,0:T(8,128)(2,1)} %param.5) | copy-start | bytes 393220
  1.5 7.0 %collective-permute-start = (bf16[8,16,128]{2,1,0:T(8,128)(2,1)S(1)}, bf16[8,16,128]{2,1,0:T(8,128)(2,1)S(1)}, u32[]{:S(2)}, u32[]{:S(2)}) collective-permute-start(bf16[8,16,128]{2,1,0:T(8,128)(2,1)S(1)} %get-tuple-element.4), channel_id=1, source_target_pairs={{1,2},{2,1},{3,4},{4,3},{5,6},{6,5},{9,10},{10,9},{11,12},{12,11},... | collective-permute-start | bytes 98312 | tf_op jit(solution)/shard_map/ppermute | solution.py:24
  6.2 5.8 %collective-permute-start.1 = (bf16[8,16,128]{2,1,0:T(8,128)(2,1)S(1)}, bf16[8,16,128]{2,1,0:T(8,128)(2,1)S(1)}, u32[]{:S(2)}, u32[]{:S(2)}) collective-permute-start(bf16[8,16,128]{2,1,0:T(8,128)(2,1)S(1)} %get-tuple-element.5), channel_id=1, source_target_pairs={{0,1},{1,0},{2,3},{3,2},{4,5},{5,4},{6,7},{7,6},{8,9},{9,8},{10,11... | collective-permute-start | bytes 98312 | tf_op jit(solution)/shard_map/ppermute | solution.py:24
  8.1 3.9 %copy-start.4 = (bf16[3,4,16,128]{3,2,1,0:T(8,128)(2,1)S(1)}, bf16[3,4,16,128]{3,2,1,0:T(8,128)(2,1)}, u32[]{:S(2)}) copy-start(bf16[3,4,16,128]{3,2,1,0:T(8,128)(2,1)} %param.6) | copy-start | bytes 147460
  12.0 17.7 %copy-start = (s32[4,2,16,128]{3,2,1,0:T(8,128)S(1)}, s32[4,2,16,128]{3,2,1,0:T(8,128)}, u32[]{:S(2)}) copy-start(s32[4,2,16,128]{3,2,1,0:T(8,128)} %base_ref.1) | copy-start | bytes 196612
  12.0 17.7 %copy-start.1 = (s32[4,64,2]{1,2,0:T(2,128)S(1)}, s32[4,64,2]{1,2,0:T(2,128)}, u32[]{:S(2)}) copy-start(s32[4,64,2]{1,2,0:T(2,128)} %param.9) | copy-start | bytes 6148
  12.0 17.7 %copy-start.2 = (s32[4,16,2]{1,2,0:T(2,128)S(1)}, s32[4,16,2]{1,2,0:T(2,128)}, u32[]{:S(2)}) copy-start(s32[4,16,2]{1,2,0:T(2,128)} %param.7) | copy-start | bytes 1540
  12.1 11.7 %collective-permute-start.5 = (bf16[60,16,128]{2,1,0:T(8,128)(2,1)S(1)}, bf16[60,16,128]{2,1,0:T(8,128)(2,1)S(1)}, u32[]{:S(2)}, u32[]{:S(2)}) collective-permute-start(bf16[60,16,128]{2,1,0:T(8,128)(2,1)S(1)} %pad_maximum_fusion.mid), channel_id=1, source_target_pairs={{16,32},{24,40},{32,16},{40,24},{48,64},{56,72},{64,48},{72,56},{8... | collective-permute-start | bytes 737288 | tf_op jit(solution)/shard_map/ppermute | solution.py:24
  15.9 8.1 %collective-permute-start.4 = (bf16[60,16,128]{2,1,0:T(8,128)(2,1)S(1)}, bf16[60,16,128]{2,1,0:T(8,128)(2,1)S(1)}, u32[]{:S(2)}, u32[]{:S(2)}) collective-permute-start(bf16[60,16,128]{2,1,0:T(8,128)(2,1)S(1)} %pad_maximum_fusion.mid), channel_id=1, source_target_pairs={{0,16},{8,24},{16,0},{24,8},{32,48},{40,56},{48,32},{56,40},{64,80... | collective-permute-start | bytes 737288 | tf_op jit(solution)/shard_map/ppermute | solution.py:24
  18.9 10.8 %collective-permute-start.3 = (bf16[60,16,128]{2,1,0:T(8,128)(2,1)S(1)}, bf16[60,16,128]{2,1,0:T(8,128)(2,1)S(1)}, u32[]{:S(2)}, u32[]{:S(2)}) collective-permute-start(bf16[60,16,128]{2,1,0:T(8,128)(2,1)S(1)} %pad_maximum_fusion.mid), channel_id=1, source_target_pairs={{8,16},{16,8},{24,32},{32,24},{40,48},{48,40},{56,64},{64,56},{72,... | collective-permute-start | bytes 737288 | tf_op jit(solution)/shard_map/ppermute | solution.py:24
  20.9 8.8 %collective-permute-start.2 = (bf16[60,16,128]{2,1,0:T(8,128)(2,1)S(1)}, bf16[60,16,128]{2,1,0:T(8,128)(2,1)S(1)}, u32[]{:S(2)}, u32[]{:S(2)}) collective-permute-start(bf16[60,16,128]{2,1,0:T(8,128)(2,1)S(1)} %pad_maximum_fusion.mid), channel_id=1, source_target_pairs={{0,8},{8,0},{16,24},{24,16},{32,40},{40,32},{48,56},{56,48},{64,72... | collective-permute-start | bytes 737288 | tf_op jit(solution)/shard_map/ppermute | solution.py:24

commit v4 on v3

--- a/solution.py
+++ b/solution.py
@@ -11,7 +11,7 @@
 CELLS = BW * BH
 QUADS = 4
 POINTS = QUADS * CELLS
-N_OFF = 5
+N_OFF = 6
 
 
 def swapped(shard, axis, first, by):
@@ -44,6 +44,7 @@
     left = column(regions[1:2], nblocks)
     mate = jnp.where((own_band & 1) == 0, 1, -1)
     paired = jnp.where((own_band & 2) == 0, 2, -2)
+    next_place = jnp.where(-2 * mate == paired, 3, 5)
     lane = lax.broadcasted_iota(jnp.int32, (nblocks, N_OFF * nblocks), 1)
     rows = []
     for quad_y in (0, 1):
@@ -53,7 +54,7 @@
             run_low = (col - starts[0]) & (nblocks - 1)
             run_high = (col - starts[1]) & (nblocks - 1)
             run = jnp.where(offset == -2, run_low, jnp.where(offset == 2, run_high, 0))
-            place = jnp.where(offset == mate, 1, jnp.where(offset == -mate, 3, 2))
+            place = jnp.where(offset == mate, 1, jnp.where(offset == -mate, next_place, 2))
             place = jnp.where(offset == paired, 4, jnp.where(offset == -paired, 0, place))
             slot = jnp.where(run < nblocks // 2, place * nblocks + col, -1)
             rows.append(jnp.where(lane == slot, 1.0, 0.0).astype(jnp.bfloat16))
@@ -72,20 +73,16 @@
     return picked
 
 
-def class_order(log_step):
+def class_order(log_step, zero):
     step = 1 << log_step
     mask = step - 1
-    source = lax.broadcasted_iota(jnp.int32, (POINTS, 128), 0)
-    lane = lax.broadcasted_iota(jnp.int32, (POINTS, 128), 1)
+    source = lax.broadcasted_iota(jnp.int32, (POINTS, POINTS), 0) + zero
+    lane = lax.broadcasted_iota(jnp.int32, (POINTS, POINTS), 1)
     x = (source & (BW - 1)) + ((source >> 7) & 1) * BW
     y = ((source >> 4) & (BH - 1)) + (source >> 8) * BH
     kind = (y & mask) * step + (x & mask)
     place = (y >> log_step) * (2 * BW // step) + (x >> log_step)
-    dest = kind * (POINTS // (step * step)) + place
-    cols = [
-        jnp.where(dest == lane + v * 128, 1.0, 0.0).astype(jnp.bfloat16) for v in range(QUADS)
-    ]
-    return jnp.concatenate(cols, axis=1)
+    return (kind * (POINTS // (step * step)) + place == lane).astype(jnp.bfloat16)
 
 
 def sort_rows(picked, nblocks, lanes_at):
@@ -122,9 +119,12 @@
     far_ref,
     regions_ref,
     base_ref,
+    order1_ref,
+    order2_ref,
     mate,
     cross,
     even2,
+    relay,
     odd2,
     mid,
     new_ref,
@@ -144,7 +144,7 @@
         selectors(regions_ref[k], run_starts(far_ref[k], own), own, nblocks)
         for k in range(ITERS + 1)
     ]
-    bands = (odd2, mate, mid, cross, even2)
+    bands = (odd2, mate, mid, cross, even2, relay)
 
     def stacked(row):
         return jnp.concatenate([b[row] for b in bands], axis=0)
@@ -163,7 +163,7 @@
                 at = (k * n_field + i + half) * nblocks
                 wind_rows[at : at + nblocks, :] = sort_rows(part, nblocks, half * CELLS)
     wind_patch[...] = jnp.dot(
-        wind_rows[...], class_order(1), preferred_element_type=jnp.float32
+        wind_rows[...], order1_ref[...], preferred_element_type=jnp.float32
     ).astype(jnp.bfloat16)
     for t in range(n_tracer):
         levels = [stacked(n_field + t * n_level + l) for l in range(n_level)]
@@ -180,7 +180,7 @@
                 at = (t * n_ext + e + half) * nblocks
                 rows_ref[at : at + nblocks, :] = sort_rows(picked, nblocks, half * CELLS)
     patch_ref[...] = jnp.dot(
-        rows_ref[...], class_order(2), preferred_element_type=jnp.float32
+        rows_ref[...], order2_ref[...], preferred_element_type=jnp.float32
     ).astype(jnp.bfloat16)
     displace = [[None] * n_comp for _ in range(n_level)]
     for k in range(ITERS):
@@ -266,7 +266,7 @@
             new_ref[t, l] = total.astype(jnp.bfloat16)
         return carry
 
-    lax.fori_loop(0, n_tracer, one_tracer, 0)
+    lax.fori_loop(0, n_tracer, one_tracer, 0, unroll=4)
 
 
 def body(tracers, wind_field, regions, stencil_base, far_start):
@@ -290,8 +290,13 @@
     )
     odd2 = swapped(packet, "tile", 2, 2)
     even2 = swapped(packet, "tile", 0, 2)
-    cross = swapped(packet, "tile", 1, 1)
+    n_bands = lax.axis_size("tile")
+    pairs = [(i, i ^ 3) for i in range(n_bands) if i % 4 in (1, 2)]
+    cross = lax.ppermute(packet, "tile", pairs)
+    pairs = [(i, i ^ 1) for i in range(2, n_bands - 2) if i % 4 in (1, 2)]
+    relay = lax.ppermute(odd2, "tile", pairs)
     mate = swapped(packet, "tile", 0, 1)
+    _, zero = lax.optimization_barrier((packet[0, 0], jnp.int32(0)))
     wind_rows = ITERS * n_comp * n_level * nblocks
     rows = n_tracer * (n_level + 2) * nblocks
     vmem = pl.BlockSpec(memory_space=pltpu.VMEM)
@@ -302,7 +307,7 @@
             jax.ShapeDtypeStruct(tracers.shape, jnp.bfloat16),
             jax.ShapeDtypeStruct(wind_field.shape, jnp.float32),
         ),
-        in_specs=[vmem] * 8,
+        in_specs=[vmem] * 11,
         out_specs=(vmem, vmem),
         scratch_shapes=[
             pltpu.VMEM((wind_rows, POINTS), jnp.bfloat16),
@@ -312,14 +317,17 @@
             pltpu.VMEM((16, n_level, nblocks, cells), jnp.float32),
             pltpu.VMEM((n_level, 3, nblocks, cells), jnp.float32),
         ],
-        compiler_params=pltpu.CompilerParams(vmem_limit_bytes=40 * 1024 * 1024),
+        compiler_params=pltpu.CompilerParams(vmem_limit_bytes=16 * 1024 * 1024),
     )(
         jnp.swapaxes(far_start, 1, 2),
         jnp.swapaxes(regions, 1, 2),
         stencil_base,
+        class_order(1, zero),
+        class_order(2, zero),
         mate,
         cross,
         even2,
+        relay,
         odd2,
         packet,
     )

time: 34.2 us -> 32.3 us (0.944)
  the two profiles are of different devices: /device:TPU:280 before, /device:TPU:409 now
where the time goes in v4:
time: 32.3 us; the launch traced here: 32 us
  starting transfers between devices  22.9 us (71%)
  Pallas kernels  3.63 us (11%)
  waiting for transfers between devices  3.43 us (11%)
  other arithmetic  1.19 us (4%)
  between operations  0.83 us (3%)
    ppermute x5, starting transfers between devices, swapped(): return lax.ppermute(shard, axis, pairs)  14.6 us
    ppermute x1, starting transfers between devices, body(): cross = lax.ppermute(packet, 'tile', pairs)  5.91 us
    pallas_call x1, Pallas kernels, body(): pl.pallas_call(transport_kernel, name='transport', out_shape=(jax.ShapeDt...  3.63 us
    ppermute x5, waiting for transfers between devices, swapped(): return lax.ppermute(shard, axis, pairs)  2.71 us
    ppermute x1, starting transfers between devices, body(): relay = lax.ppermute(odd2, 'tile', pairs)  2.42 us
    select_n x1, other arithmetic, body(): got_odd = swapped(jnp.where(even, bottom, top), 'lev', 1, 1)  0.82 us
    ppermute x1, waiting for transfers between devices, body(): relay = lax.ppermute(odd2, 'tile', pairs)  0.72 us
  transfers between devices with their start and end apart: 7, of which 2 were waited for; matrix products, arithmetic and copies ran while one was open for 1% of the time, Pallas kernels for 0%

profile of v4, /device:TPU:409, one launch (start us, length us, event | category | flops | bytes accessed | tf_op | source)
XLA Modules:
  0.0 32.0 jit_solution(8678695815592859224)
XLA Ops:
  0.6 0.0 copy-start.3
  0.7 0.8 %bitcast_select_fusion.2 = (bf16[8,16,128]{2,1,0:T(8,128)(2,1)S(1)}, bf16[8,16,128]{2,1,0:T(8,128)(2,1)S(1)}) fusion(pred[]{:T(512)S(6)} %eq.20, bf16[8,4,16,128]{3,2,1,0:T(8,128)(2,1)} %param.5), kind=kLoop, calls=%fused_computation.7 | loop fusion | flops 32768 | bytes 131073 | tf_op jit(solution)/shard_map/jit(_where)/select_n | solution.py:278
  1.5 4.4 %collective-permute-start = (bf16[8,16,128]{2,1,0:T(8,128)(2,1)S(1)}, bf16[8,16,128]{2,1,0:T(8,128)(2,1)S(1)}, u32[]{:S(2)}, u32[]{:S(2)}) collective-permute-start(bf16[8,16,128]{2,1,0:T(8,128)(2,1)S(1)} %get-tuple-element.4), channel_id=1, source_target_pairs={{1,2},{2,1},{3,4},{4,3},{5,6},{6,5},{9,10},{10,9},{11,12},{12,11},... | collective-permute-start | bytes 98312 | tf_op jit(solution)/shard_map/ppermute | solution.py:24
  5.9 1.9 %collective-permute-start.1 = (bf16[8,16,128]{2,1,0:T(8,128)(2,1)S(1)}, bf16[8,16,128]{2,1,0:T(8,128)(2,1)S(1)}, u32[]{:S(2)}, u32[]{:S(2)}) collective-permute-start(bf16[8,16,128]{2,1,0:T(8,128)(2,1)S(1)} %get-tuple-element.5), channel_id=1, source_target_pairs={{0,1},{1,0},{2,3},{3,2},{4,5},{5,4},{6,7},{7,6},{8,9},{9,8},{10,11... | collective-permute-start | bytes 98312 | tf_op jit(solution)/shard_map/ppermute | solution.py:24
  7.8 0.0 copy-start.4
  7.8 0.0 collective-permute-done
  7.9 2.7 %collective-permute-done.1 = bf16[8,16,128]{2,1,0:T(8,128)(2,1)S(1)} collective-permute-done((bf16[8,16,128]{2,1,0:T(8,128)(2,1)S(1)}, bf16[8,16,128]{2,1,0:T(8,128)(2,1)S(1)}, u32[]{:S(2)}, u32[]{:S(2)}) %collective-permute-start.1) | collective-permute-done | bytes 32800 | tf_op jit(solution)/shard_map/ppermute | solution.py:24
  10.6 0.0 copy-done.3
  10.6 0.0 copy-done.4
  10.6 4.4 %collective-permute-start.5 = (bf16[60,16,128]{2,1,0:T(8,128)(2,1)S(1)}, bf16[60,16,128]{2,1,0:T(8,128)(2,1)S(1)}, u32[]{:S(2)}, u32[]{:S(2)}) collective-permute-start(bf16[60,16,128]{2,1,0:T(8,128)(2,1)S(1)} %pad_maximum_fusion.mid), channel_id=1, source_target_pairs={{16,32},{24,40},{32,16},{40,24},{48,64},{56,72},{64,48},{72,56},{8... | collective-permute-start | bytes 737288 | tf_op jit(solution)/shard_map/ppermute | solution.py:24
  15.0 1.9 %collective-permute-start.4 = (bf16[60,16,128]{2,1,0:T(8,128)(2,1)S(1)}, bf16[60,16,128]{2,1,0:T(8,128)(2,1)S(1)}, u32[]{:S(2)}, u32[]{:S(2)}) collective-permute-start(bf16[60,16,128]{2,1,0:T(8,128)(2,1)S(1)} %pad_maximum_fusion.mid), channel_id=1, source_target_pairs={{0,16},{8,24},{16,0},{24,8},{32,48},{40,56},{48,32},{56,40},{64,80... | collective-permute-start | bytes 737288 | tf_op jit(solution)/shard_map/ppermute | solution.py:24
  17.0 5.9 %collective-permute-start.3 = (bf16[60,16,128]{2,1,0:T(8,128)(2,1)S(1)}, bf16[60,16,128]{2,1,0:T(8,128)(2,1)S(1)}, u32[]{:S(2)}, u32[]{:S(2)}) collective-permute-start(bf16[60,16,128]{2,1,0:T(8,128)(2,1)S(1)} %pad_maximum_fusion.mid), channel_id=1, source_target_pairs={{8,16},{16,8},{40,48},{48,40},{72,80},{80,72},{104,112},{112,104},... | collective-permute-start | bytes 737288 | tf_op jit(solution)/shard_map/ppermute | solution.py:295
  22.9 1.9 %collective-permute-start.2 = (bf16[60,16,128]{2,1,0:T(8,128)(2,1)S(1)}, bf16[60,16,128]{2,1,0:T(8,128)(2,1)S(1)}, u32[]{:S(2)}, u32[]{:S(2)}) collective-permute-start(bf16[60,16,128]{2,1,0:T(8,128)(2,1)S(1)} %pad_maximum_fusion.mid), channel_id=1, source_target_pairs={{0,8},{8,0},{16,24},{24,16},{32,40},{40,32},{48,56},{56,48},{64,72... | collective-permute-start | bytes 737288 | tf_op jit(solution)/shard_map/ppermute | solution.py:24
  24.8 0.0 collective-permute-done.5.odd2
  24.8 2.4 %collective-permute-start.6 = (bf16[60,16,128]{2,1,0:T(8,128)(2,1)S(1)}, bf16[60,16,128]{2,1,0:T(8,128)(2,1)S(1)}, u32[]{:S(2)}, u32[]{:S(2)}) collective-permute-start(bf16[60,16,128]{2,1,0:T(8,128)(2,1)S(1)} %collective-permute-done.5.odd2), channel_id=1, source_target_pairs={{16,24},{40,32},{48,56},{72,64},{80,88},{104,96},{112,120},{136,12... | collective-permute-start | bytes 737288 | tf_op jit(solution)/shard_map/ppermute | solution.py:297
  27.2 0.2 fusion.1.order2_ref
  27.4 0.0 copy-start
  27.4 0.0 copy-start.1
  27.4 0.0 copy-start.2
  27.4 0.2 fusion.order1_ref
  27.6 0.0 collective-permute-done.4.even2
  27.6 0.0 collective-permute-done.3.cross
  27.6 0.0 collective-permute-done.2.mate
  27.6 0.7 %collective-permute-done.6.relay = bf16[60,16,128]{2,1,0:T(8,128)(2,1)S(1)} collective-permute-done((bf16[60,16,128]{2,1,0:T(8,128)(2,1)S(1)}, bf16[60,16,128]{2,1,0:T(8,128)(2,1)S(1)}, u32[]{:S(2)}, u32[]{:S(2)}) %collective-permute-start.6) | collective-permute-done | bytes 245792 | tf_op jit(solution)/shard_map/ppermute | solution.py:297
  28.4 0.0 copy-done
  28.4 0.0 copy-done.1
  28.4 0.0 copy-done.2
  28.4 3.6 %transport.1 = (bf16[8,4,16,128]{3,2,1,0:T(8,128)(2,1)}, f32[3,4,16,128]{3,2,1,0:T(8,128)}) custom-call(s32[4,2,64]{2,1,0:T(2,128)S(1)} %bitcast.16, s32[4,2,16]{2,1,0:T(2,128)S(1)} %bitcast.17, s32[4,2,16,128]{3,2,1,0:T(8,128)S(1)} %copy-done, bf16[512,512]{1,0:T(8,128)(2,1)S(1)} %fusion.order1_ref, bf16[512,512]{1,0:T(8,128)(2,1)S(1)} %fusion.1.order2_ref, ...), custom_call_target="tpu_custom_call" | custom-call | tf_op jit(solution)/shard_map/transport/pallas_call | solution.py:303
  (3 shorter events, 0.1 us)
Async XLA Ops:
  0.6 9.9 %copy-start.3 = (bf16[8,4,16,128]{3,2,1,0:T(8,128)(2,1)S(1)}, bf16[8,4,16,128]{3,2,1,0:T(8,128)(2,1)}, u32[]{:S(2)}) copy-start(bf16[8,4,16,128]{3,2,1,0:T(8,128)(2,1)} %param.5) | copy-start | bytes 393220
  1.5 6.4 %collective-permute-start = (bf16[8,16,128]{2,1,0:T(8,128)(2,1)S(1)}, bf16[8,16,128]{2,1,0:T(8,128)(2,1)S(1)}, u32[]{:S(2)}, u32[]{:S(2)}) collective-permute-start(bf16[8,16,128]{2,1,0:T(8,128)(2,1)S(1)} %get-tuple-element.4), channel_id=1, source_target_pairs={{1,2},{2,1},{3,4},{4,3},{5,6},{6,5},{9,10},{10,9},{11,12},{12,11},... | collective-permute-start | bytes 98312 | tf_op jit(solution)/shard_map/ppermute | solution.py:24
  5.9 4.7 %collective-permute-start.1 = (bf16[8,16,128]{2,1,0:T(8,128)(2,1)S(1)}, bf16[8,16,128]{2,1,0:T(8,128)(2,1)S(1)}, u32[]{:S(2)}, u32[]{:S(2)}) collective-permute-start(bf16[8,16,128]{2,1,0:T(8,128)(2,1)S(1)} %get-tuple-element.5), channel_id=1, source_target_pairs={{0,1},{1,0},{2,3},{3,2},{4,5},{5,4},{6,7},{7,6},{8,9},{9,8},{10,11... | collective-permute-start | bytes 98312 | tf_op jit(solution)/shard_map/ppermute | solution.py:24
  7.8 2.7 %copy-start.4 = (bf16[3,4,16,128]{3,2,1,0:T(8,128)(2,1)S(1)}, bf16[3,4,16,128]{3,2,1,0:T(8,128)(2,1)}, u32[]{:S(2)}) copy-start(bf16[3,4,16,128]{3,2,1,0:T(8,128)(2,1)} %param.6) | copy-start | bytes 147460
  10.6 14.2 %collective-permute-start.5 = (bf16[60,16,128]{2,1,0:T(8,128)(2,1)S(1)}, bf16[60,16,128]{2,1,0:T(8,128)(2,1)S(1)}, u32[]{:S(2)}, u32[]{:S(2)}) collective-permute-start(bf16[60,16,128]{2,1,0:T(8,128)(2,1)S(1)} %pad_maximum_fusion.mid), channel_id=1, source_target_pairs={{16,32},{24,40},{32,16},{40,24},{48,64},{56,72},{64,48},{72,56},{8... | collective-permute-start | bytes 737288 | tf_op jit(solution)/shard_map/ppermute | solution.py:24
  15.0 12.6 %collective-permute-start.4 = (bf16[60,16,128]{2,1,0:T(8,128)(2,1)S(1)}, bf16[60,16,128]{2,1,0:T(8,128)(2,1)S(1)}, u32[]{:S(2)}, u32[]{:S(2)}) collective-permute-start(bf16[60,16,128]{2,1,0:T(8,128)(2,1)S(1)} %pad_maximum_fusion.mid), channel_id=1, source_target_pairs={{0,16},{8,24},{16,0},{24,8},{32,48},{40,56},{48,32},{56,40},{64,80... | collective-permute-start | bytes 737288 | tf_op jit(solution)/shard_map/ppermute | solution.py:24
  17.0 10.7 %collective-permute-start.3 = (bf16[60,16,128]{2,1,0:T(8,128)(2,1)S(1)}, bf16[60,16,128]{2,1,0:T(8,128)(2,1)S(1)}, u32[]{:S(2)}, u32[]{:S(2)}) collective-permute-start(bf16[60,16,128]{2,1,0:T(8,128)(2,1)S(1)} %pad_maximum_fusion.mid), channel_id=1, source_target_pairs={{8,16},{16,8},{40,48},{48,40},{72,80},{80,72},{104,112},{112,104},... | collective-permute-start | bytes 737288 | tf_op jit(solution)/shard_map/ppermute | solution.py:295
  22.9 4.7 %collective-permute-start.2 = (bf16[60,16,128]{2,1,0:T(8,128)(2,1)S(1)}, bf16[60,16,128]{2,1,0:T(8,128)(2,1)S(1)}, u32[]{:S(2)}, u32[]{:S(2)}) collective-permute-start(bf16[60,16,128]{2,1,0:T(8,128)(2,1)S(1)} %pad_maximum_fusion.mid), channel_id=1, source_target_pairs={{0,8},{8,0},{16,24},{24,16},{32,40},{40,32},{48,56},{56,48},{64,72... | collective-permute-start | bytes 737288 | tf_op jit(solution)/shard_map/ppermute | solution.py:24
  24.8 3.5 %collective-permute-start.6 = (bf16[60,16,128]{2,1,0:T(8,128)(2,1)S(1)}, bf16[60,16,128]{2,1,0:T(8,128)(2,1)S(1)}, u32[]{:S(2)}, u32[]{:S(2)}) collective-permute-start(bf16[60,16,128]{2,1,0:T(8,128)(2,1)S(1)} %collective-permute-done.5.odd2), channel_id=1, source_target_pairs={{16,24},{40,32},{48,56},{72,64},{80,88},{104,96},{112,120},{136,12... | collective-permute-start | bytes 737288 | tf_op jit(solution)/shard_map/ppermute | solution.py:297
  27.4 0.9 %copy-start = (s32[4,2,16,128]{3,2,1,0:T(8,128)S(1)}, s32[4,2,16,128]{3,2,1,0:T(8,128)}, u32[]{:S(2)}) copy-start(s32[4,2,16,128]{3,2,1,0:T(8,128)} %base_ref.1) | copy-start | bytes 196612
  27.4 0.9 %copy-start.1 = (s32[4,64,2]{1,2,0:T(2,128)S(1)}, s32[4,64,2]{1,2,0:T(2,128)}, u32[]{:S(2)}) copy-start(s32[4,64,2]{1,2,0:T(2,128)} %param.9) | copy-start | bytes 6148
  27.4 0.9 %copy-start.2 = (s32[4,16,2]{1,2,0:T(2,128)S(1)}, s32[4,16,2]{1,2,0:T(2,128)}, u32[]{:S(2)}) copy-start(s32[4,16,2]{1,2,0:T(2,128)} %param.7) | copy-start | bytes 1540

commit v5 on v4

--- a/solution.py
+++ b/solution.py
@@ -277,8 +277,9 @@
     bottom, top = tracers[:, 0], tracers[:, n_level - 1]
     got_odd = swapped(jnp.where(even, bottom, top), "lev", 1, 1)
     got_even = swapped(jnp.where(even, top, bottom), "lev", 0, 1)
-    below = jnp.where(even, got_odd, got_even)
-    above = jnp.where(even, got_even, got_odd)
+    odd = level_pos % 2 == 1
+    below = jnp.where(odd, got_even, got_odd)
+    above = jnp.where(odd, got_odd, got_even)
     packet = jnp.concatenate(
         [
             wind_field.reshape(-1, nblocks, cells),

time: 32.3 us -> 31.4 us (0.972)
  the two profiles are of different devices: /device:TPU:409 before, /device:TPU:417 now
where the time goes in v5:
time: 31.4 us; the launch traced here: 31.1 us
  starting transfers between devices  20.8 us (66%)
  waiting for transfers between devices  4.65 us (15%)
  Pallas kernels  3.63 us (12%)
  other arithmetic  1.19 us (4%)
  between operations  0.83 us (3%)
    ppermute x5, starting transfers between devices, swapped(): return lax.ppermute(shard, axis, pairs)  12.4 us
    ppermute x1, starting transfers between devices, body(): cross = lax.ppermute(packet, 'tile', pairs)  5.91 us
    ppermute x5, waiting for transfers between devices, swapped(): return lax.ppermute(shard, axis, pairs)  3.93 us
    pallas_call x1, Pallas kernels, body(): pl.pallas_call(transport_kernel, name='transport', out_shape=(jax.ShapeDt...  3.63 us
    ppermute x1, starting transfers between devices, body(): relay = lax.ppermute(odd2, 'tile', pairs)  2.42 us
    select_n x1, other arithmetic, body(): got_even = swapped(jnp.where(even, top, bottom), 'lev', 0, 1)  0.82 us
    ppermute x1, waiting for transfers between devices, body(): relay = lax.ppermute(odd2, 'tile', pairs)  0.72 us
  transfers between devices with their start and end apart: 7, of which 3 were waited for; matrix products, arithmetic and copies ran while one was open for 1% of the time, Pallas kernels for 0%

profile of v5, /device:TPU:417, one launch (start us, length us, event | category | flops | bytes accessed | tf_op | source)
XLA Modules:
  0.0 31.1 jit_solution(12838659651303092346)
XLA Ops:
  0.6 0.0 copy-start.3
  0.7 0.8 %bitcast_select_fusion.2 = (bf16[8,16,128]{2,1,0:T(8,128)(2,1)S(1)}, bf16[8,16,128]{2,1,0:T(8,128)(2,1)S(1)}) fusion(pred[]{:T(512)S(6)} %eq.25, bf16[8,4,16,128]{3,2,1,0:T(8,128)(2,1)} %param.5), kind=kLoop, calls=%fused_computation.7 | loop fusion | flops 32768 | bytes 131073 | tf_op jit(solution)/shard_map/jit(_where)/select_n | solution.py:279
  1.5 2.3 %collective-permute-start = (bf16[8,16,128]{2,1,0:T(8,128)(2,1)S(1)}, bf16[8,16,128]{2,1,0:T(8,128)(2,1)S(1)}, u32[]{:S(2)}, u32[]{:S(2)}) collective-permute-start(bf16[8,16,128]{2,1,0:T(8,128)(2,1)S(1)} %get-tuple-element.4), channel_id=1, source_target_pairs={{0,1},{1,0},{2,3},{3,2},{4,5},{5,4},{6,7},{7,6},{8,9},{9,8},{10,11... | collective-permute-start | bytes 98312 | tf_op jit(solution)/shard_map/ppermute | solution.py:24
  3.8 1.9 %collective-permute-start.1 = (bf16[8,16,128]{2,1,0:T(8,128)(2,1)S(1)}, bf16[8,16,128]{2,1,0:T(8,128)(2,1)S(1)}, u32[]{:S(2)}, u32[]{:S(2)}) collective-permute-start(bf16[8,16,128]{2,1,0:T(8,128)(2,1)S(1)} %get-tuple-element.5), channel_id=1, source_target_pairs={{1,2},{2,1},{3,4},{4,3},{5,6},{6,5},{9,10},{10,9},{11,12},{12,11},... | collective-permute-start | bytes 98312 | tf_op jit(solution)/shard_map/ppermute | solution.py:24
  5.7 0.0 copy-start.4
  5.7 0.4 %collective-permute-done = bf16[8,16,128]{2,1,0:T(8,128)(2,1)S(1)} collective-permute-done((bf16[8,16,128]{2,1,0:T(8,128)(2,1)S(1)}, bf16[8,16,128]{2,1,0:T(8,128)(2,1)S(1)}, u32[]{:S(2)}, u32[]{:S(2)}) %collective-permute-start) | collective-permute-done | bytes 32800 | tf_op jit(solution)/shard_map/ppermute | solution.py:24
  6.1 3.5 %collective-permute-done.1 = bf16[8,16,128]{2,1,0:T(8,128)(2,1)S(1)} collective-permute-done((bf16[8,16,128]{2,1,0:T(8,128)(2,1)S(1)}, bf16[8,16,128]{2,1,0:T(8,128)(2,1)S(1)}, u32[]{:S(2)}, u32[]{:S(2)}) %collective-permute-start.1) | collective-permute-done | bytes 32800 | tf_op jit(solution)/shard_map/ppermute | solution.py:24
  9.7 0.0 copy-done.3
  9.7 0.0 copy-done.4
  9.7 4.4 %collective-permute-start.5 = (bf16[60,16,128]{2,1,0:T(8,128)(2,1)S(1)}, bf16[60,16,128]{2,1,0:T(8,128)(2,1)S(1)}, u32[]{:S(2)}, u32[]{:S(2)}) collective-permute-start(bf16[60,16,128]{2,1,0:T(8,128)(2,1)S(1)} %pad_maximum_fusion.mid), channel_id=1, source_target_pairs={{16,32},{24,40},{32,16},{40,24},{48,64},{56,72},{64,48},{72,56},{8... | collective-permute-start | bytes 737288 | tf_op jit(solution)/shard_map/ppermute | solution.py:24
  14.1 1.9 %collective-permute-start.4 = (bf16[60,16,128]{2,1,0:T(8,128)(2,1)S(1)}, bf16[60,16,128]{2,1,0:T(8,128)(2,1)S(1)}, u32[]{:S(2)}, u32[]{:S(2)}) collective-permute-start(bf16[60,16,128]{2,1,0:T(8,128)(2,1)S(1)} %pad_maximum_fusion.mid), channel_id=1, source_target_pairs={{0,16},{8,24},{16,0},{24,8},{32,48},{40,56},{48,32},{56,40},{64,80... | collective-permute-start | bytes 737288 | tf_op jit(solution)/shard_map/ppermute | solution.py:24
  16.1 5.9 %collective-permute-start.3 = (bf16[60,16,128]{2,1,0:T(8,128)(2,1)S(1)}, bf16[60,16,128]{2,1,0:T(8,128)(2,1)S(1)}, u32[]{:S(2)}, u32[]{:S(2)}) collective-permute-start(bf16[60,16,128]{2,1,0:T(8,128)(2,1)S(1)} %pad_maximum_fusion.mid), channel_id=1, source_target_pairs={{8,16},{16,8},{40,48},{48,40},{72,80},{80,72},{104,112},{112,104},... | collective-permute-start | bytes 737288 | tf_op jit(solution)/shard_map/ppermute | solution.py:296
  22.0 1.9 %collective-permute-start.2 = (bf16[60,16,128]{2,1,0:T(8,128)(2,1)S(1)}, bf16[60,16,128]{2,1,0:T(8,128)(2,1)S(1)}, u32[]{:S(2)}, u32[]{:S(2)}) collective-permute-start(bf16[60,16,128]{2,1,0:T(8,128)(2,1)S(1)} %pad_maximum_fusion.mid), channel_id=1, source_target_pairs={{0,8},{8,0},{16,24},{24,16},{32,40},{40,32},{48,56},{56,48},{64,72... | collective-permute-start | bytes 737288 | tf_op jit(solution)/shard_map/ppermute | solution.py:24
  23.9 0.0 collective-permute-done.5.odd2
  23.9 2.4 %collective-permute-start.6 = (bf16[60,16,128]{2,1,0:T(8,128)(2,1)S(1)}, bf16[60,16,128]{2,1,0:T(8,128)(2,1)S(1)}, u32[]{:S(2)}, u32[]{:S(2)}) collective-permute-start(bf16[60,16,128]{2,1,0:T(8,128)(2,1)S(1)} %collective-permute-done.5.odd2), channel_id=1, source_target_pairs={{16,24},{40,32},{48,56},{72,64},{80,88},{104,96},{112,120},{136,12... | collective-permute-start | bytes 737288 | tf_op jit(solution)/shard_map/ppermute | solution.py:298
  26.3 0.2 fusion.1.order2_ref
  26.5 0.0 copy-start
  26.5 0.0 copy-start.1
  26.5 0.0 copy-start.2
  26.5 0.2 fusion.order1_ref
  26.7 0.0 collective-permute-done.4.even2
  26.7 0.0 collective-permute-done.3.cross
  26.7 0.0 collective-permute-done.2.mate
  26.7 0.7 %collective-permute-done.6.relay = bf16[60,16,128]{2,1,0:T(8,128)(2,1)S(1)} collective-permute-done((bf16[60,16,128]{2,1,0:T(8,128)(2,1)S(1)}, bf16[60,16,128]{2,1,0:T(8,128)(2,1)S(1)}, u32[]{:S(2)}, u32[]{:S(2)}) %collective-permute-start.6) | collective-permute-done | bytes 245792 | tf_op jit(solution)/shard_map/ppermute | solution.py:298
  27.5 0.0 copy-done
  27.5 0.0 copy-done.1
  27.5 0.0 copy-done.2
  27.5 3.6 %transport.1 = (bf16[8,4,16,128]{3,2,1,0:T(8,128)(2,1)}, f32[3,4,16,128]{3,2,1,0:T(8,128)}) custom-call(s32[4,2,64]{2,1,0:T(2,128)S(1)} %bitcast.16, s32[4,2,16]{2,1,0:T(2,128)S(1)} %bitcast.17, s32[4,2,16,128]{3,2,1,0:T(8,128)S(1)} %copy-done, bf16[512,512]{1,0:T(8,128)(2,1)S(1)} %fusion.order1_ref, bf16[512,512]{1,0:T(8,128)(2,1)S(1)} %fusion.1.order2_ref, ...), custom_call_target="tpu_custom_call" | custom-call | tf_op jit(solution)/shard_map/transport/pallas_call | solution.py:304
  (3 shorter events, 0.1 us)
Async XLA Ops:
  0.6 9.0 %copy-start.3 = (bf16[8,4,16,128]{3,2,1,0:T(8,128)(2,1)S(1)}, bf16[8,4,16,128]{3,2,1,0:T(8,128)(2,1)}, u32[]{:S(2)}) copy-start(bf16[8,4,16,128]{3,2,1,0:T(8,128)(2,1)} %param.5) | copy-start | bytes 393220
  1.5 4.7 %collective-permute-start = (bf16[8,16,128]{2,1,0:T(8,128)(2,1)S(1)}, bf16[8,16,128]{2,1,0:T(8,128)(2,1)S(1)}, u32[]{:S(2)}, u32[]{:S(2)}) collective-permute-start(bf16[8,16,128]{2,1,0:T(8,128)(2,1)S(1)} %get-tuple-element.4), channel_id=1, source_target_pairs={{0,1},{1,0},{2,3},{3,2},{4,5},{5,4},{6,7},{7,6},{8,9},{9,8},{10,11... | collective-permute-start | bytes 98312 | tf_op jit(solution)/shard_map/ppermute | solution.py:24
  3.8 5.9 %collective-permute-start.1 = (bf16[8,16,128]{2,1,0:T(8,128)(2,1)S(1)}, bf16[8,16,128]{2,1,0:T(8,128)(2,1)S(1)}, u32[]{:S(2)}, u32[]{:S(2)}) collective-permute-start(bf16[8,16,128]{2,1,0:T(8,128)(2,1)S(1)} %get-tuple-element.5), channel_id=1, source_target_pairs={{1,2},{2,1},{3,4},{4,3},{5,6},{6,5},{9,10},{10,9},{11,12},{12,11},... | collective-permute-start | bytes 98312 | tf_op jit(solution)/shard_map/ppermute | solution.py:24
  5.7 4.0 %copy-start.4 = (bf16[3,4,16,128]{3,2,1,0:T(8,128)(2,1)S(1)}, bf16[3,4,16,128]{3,2,1,0:T(8,128)(2,1)}, u32[]{:S(2)}) copy-start(bf16[3,4,16,128]{3,2,1,0:T(8,128)(2,1)} %param.6) | copy-start | bytes 147460
  9.7 14.2 %collective-permute-start.5 = (bf16[60,16,128]{2,1,0:T(8,128)(2,1)S(1)}, bf16[60,16,128]{2,1,0:T(8,128)(2,1)S(1)}, u32[]{:S(2)}, u32[]{:S(2)}) collective-permute-start(bf16[60,16,128]{2,1,0:T(8,128)(2,1)S(1)} %pad_maximum_fusion.mid), channel_id=1, source_target_pairs={{16,32},{24,40},{32,16},{40,24},{48,64},{56,72},{64,48},{72,56},{8... | collective-permute-start | bytes 737288 | tf_op jit(solution)/shard_map/ppermute | solution.py:24
  14.1 12.6 %collective-permute-start.4 = (bf16[60,16,128]{2,1,0:T(8,128)(2,1)S(1)}, bf16[60,16,128]{2,1,0:T(8,128)(2,1)S(1)}, u32[]{:S(2)}, u32[]{:S(2)}) collective-permute-start(bf16[60,16,128]{2,1,0:T(8,128)(2,1)S(1)} %pad_maximum_fusion.mid), channel_id=1, source_target_pairs={{0,16},{8,24},{16,0},{24,8},{32,48},{40,56},{48,32},{56,40},{64,80... | collective-permute-start | bytes 737288 | tf_op jit(solution)/shard_map/ppermute | solution.py:24
  16.1 10.7 %collective-permute-start.3 = (bf16[60,16,128]{2,1,0:T(8,128)(2,1)S(1)}, bf16[60,16,128]{2,1,0:T(8,128)(2,1)S(1)}, u32[]{:S(2)}, u32[]{:S(2)}) collective-permute-start(bf16[60,16,128]{2,1,0:T(8,128)(2,1)S(1)} %pad_maximum_fusion.mid), channel_id=1, source_target_pairs={{8,16},{16,8},{40,48},{48,40},{72,80},{80,72},{104,112},{112,104},... | collective-permute-start | bytes 737288 | tf_op jit(solution)/shard_map/ppermute | solution.py:296
  22.0 4.7 %collective-permute-start.2 = (bf16[60,16,128]{2,1,0:T(8,128)(2,1)S(1)}, bf16[60,16,128]{2,1,0:T(8,128)(2,1)S(1)}, u32[]{:S(2)}, u32[]{:S(2)}) collective-permute-start(bf16[60,16,128]{2,1,0:T(8,128)(2,1)S(1)} %pad_maximum_fusion.mid), channel_id=1, source_target_pairs={{0,8},{8,0},{16,24},{24,16},{32,40},{40,32},{48,56},{56,48},{64,72... | collective-permute-start | bytes 737288 | tf_op jit(solution)/shard_map/ppermute | solution.py:24
  23.9 3.5 %collective-permute-start.6 = (bf16[60,16,128]{2,1,0:T(8,128)(2,1)S(1)}, bf16[60,16,128]{2,1,0:T(8,128)(2,1)S(1)}, u32[]{:S(2)}, u32[]{:S(2)}) collective-permute-start(bf16[60,16,128]{2,1,0:T(8,128)(2,1)S(1)} %collective-permute-done.5.odd2), channel_id=1, source_target_pairs={{16,24},{40,32},{48,56},{72,64},{80,88},{104,96},{112,120},{136,12... | collective-permute-start | bytes 737288 | tf_op jit(solution)/shard_map/ppermute | solution.py:298
  26.5 0.9 %copy-start = (s32[4,2,16,128]{3,2,1,0:T(8,128)S(1)}, s32[4,2,16,128]{3,2,1,0:T(8,128)}, u32[]{:S(2)}) copy-start(s32[4,2,16,128]{3,2,1,0:T(8,128)} %base_ref.1) | copy-start | bytes 196612
  26.5 0.9 %copy-start.1 = (s32[4,64,2]{1,2,0:T(2,128)S(1)}, s32[4,64,2]{1,2,0:T(2,128)}, u32[]{:S(2)}) copy-start(s32[4,64,2]{1,2,0:T(2,128)} %param.9) | copy-start | bytes 6148
  26.5 0.9 %copy-start.2 = (s32[4,16,2]{1,2,0:T(2,128)S(1)}, s32[4,16,2]{1,2,0:T(2,128)}, u32[]{:S(2)}) copy-start(s32[4,16,2]{1,2,0:T(2,128)} %param.7) | copy-start | bytes 1540

commit v6 on v5

--- a/solution.py
+++ b/solution.py
@@ -121,10 +121,10 @@
     base_ref,
     order1_ref,
     order2_ref,
+    relay,
     mate,
     cross,
     even2,
-    relay,
     odd2,
     mid,
     new_ref,
@@ -325,10 +325,10 @@
         stencil_base,
         class_order(1, zero),
         class_order(2, zero),
+        relay,
         mate,
         cross,
         even2,
-        relay,
         odd2,
         packet,
     )

time: 31.4 us -> 31.4 us (level)
  no operation moved by 1% of the time
where the time goes in v6:
time: 31.4 us; the launch traced here: 31.1 us
  starting transfers between devices  20.8 us (66%)
  waiting for transfers between devices  4.65 us (15%)
  Pallas kernels  3.63 us (12%)
  other arithmetic  1.19 us (4%)
  between operations  0.83 us (3%)
    ppermute x5, starting transfers between devices, swapped(): return lax.ppermute(shard, axis, pairs)  12.4 us
    ppermute x1, starting transfers between devices, body(): cross = lax.ppermute(packet, 'tile', pairs)  5.91 us
    ppermute x5, waiting for transfers between devices, swapped(): return lax.ppermute(shard, axis, pairs)  3.93 us
    pallas_call x1, Pallas kernels, body(): pl.pallas_call(transport_kernel, name='transport', out_shape=(jax.ShapeDt...  3.63 us
    ppermute x1, starting transfers between devices, body(): relay = lax.ppermute(odd2, 'tile', pairs)  2.42 us
    select_n x1, other arithmetic, body(): got_even = swapped(jnp.where(even, top, bottom), 'lev', 0, 1)  0.82 us
    ppermute x1, waiting for transfers between devices, body(): relay = lax.ppermute(odd2, 'tile', pairs)  0.72 us
  transfers between devices with their start and end apart: 7, of which 3 were waited for; matrix products, arithmetic and copies ran while one was open for 1% of the time, Pallas kernels for 0%

profile of v6, /device:TPU:417, one launch (start us, length us, event | category | flops | bytes accessed | tf_op | source)
XLA Modules:
  0.0 31.1 jit_solution(6998359609260032718)
XLA Ops:
  0.6 0.0 copy-start.3
  0.7 0.8 %bitcast_select_fusion.2 = (bf16[8,16,128]{2,1,0:T(8,128)(2,1)S(1)}, bf16[8,16,128]{2,1,0:T(8,128)(2,1)S(1)}) fusion(pred[]{:T(512)S(6)} %eq.25, bf16[8,4,16,128]{3,2,1,0:T(8,128)(2,1)} %param.5), kind=kLoop, calls=%fused_computation.7 | loop fusion | flops 32768 | bytes 131073 | tf_op jit(solution)/shard_map/jit(_where)/select_n | solution.py:279
  1.5 2.3 %collective-permute-start = (bf16[8,16,128]{2,1,0:T(8,128)(2,1)S(1)}, bf16[8,16,128]{2,1,0:T(8,128)(2,1)S(1)}, u32[]{:S(2)}, u32[]{:S(2)}) collective-permute-start(bf16[8,16,128]{2,1,0:T(8,128)(2,1)S(1)} %get-tuple-element.4), channel_id=1, source_target_pairs={{0,1},{1,0},{2,3},{3,2},{4,5},{5,4},{6,7},{7,6},{8,9},{9,8},{10,11... | collective-permute-start | bytes 98312 | tf_op jit(solution)/shard_map/ppermute | solution.py:24
  3.8 1.9 %collective-permute-start.1 = (bf16[8,16,128]{2,1,0:T(8,128)(2,1)S(1)}, bf16[8,16,128]{2,1,0:T(8,128)(2,1)S(1)}, u32[]{:S(2)}, u32[]{:S(2)}) collective-permute-start(bf16[8,16,128]{2,1,0:T(8,128)(2,1)S(1)} %get-tuple-element.5), channel_id=1, source_target_pairs={{1,2},{2,1},{3,4},{4,3},{5,6},{6,5},{9,10},{10,9},{11,12},{12,11},... | collective-permute-start | bytes 98312 | tf_op jit(solution)/shard_map/ppermute | solution.py:24
  5.7 0.0 copy-start.4
  5.7 0.4 %collective-permute-done = bf16[8,16,128]{2,1,0:T(8,128)(2,1)S(1)} collective-permute-done((bf16[8,16,128]{2,1,0:T(8,128)(2,1)S(1)}, bf16[8,16,128]{2,1,0:T(8,128)(2,1)S(1)}, u32[]{:S(2)}, u32[]{:S(2)}) %collective-permute-start) | collective-permute-done | bytes 32800 | tf_op jit(solution)/shard_map/ppermute | solution.py:24
  6.1 3.5 %collective-permute-done.1 = bf16[8,16,128]{2,1,0:T(8,128)(2,1)S(1)} collective-permute-done((bf16[8,16,128]{2,1,0:T(8,128)(2,1)S(1)}, bf16[8,16,128]{2,1,0:T(8,128)(2,1)S(1)}, u32[]{:S(2)}, u32[]{:S(2)}) %collective-permute-start.1) | collective-permute-done | bytes 32800 | tf_op jit(solution)/shard_map/ppermute | solution.py:24
  9.7 0.0 copy-done.3
  9.7 0.0 copy-done.4
  9.7 4.4 %collective-permute-start.2 = (bf16[60,16,128]{2,1,0:T(8,128)(2,1)S(1)}, bf16[60,16,128]{2,1,0:T(8,128)(2,1)S(1)}, u32[]{:S(2)}, u32[]{:S(2)}) collective-permute-start(bf16[60,16,128]{2,1,0:T(8,128)(2,1)S(1)} %pad_maximum_fusion.mid), channel_id=1, source_target_pairs={{16,32},{24,40},{32,16},{40,24},{48,64},{56,72},{64,48},{72,56},{8... | collective-permute-start | bytes 737288 | tf_op jit(solution)/shard_map/ppermute | solution.py:24
  14.1 1.9 %collective-permute-start.6 = (bf16[60,16,128]{2,1,0:T(8,128)(2,1)S(1)}, bf16[60,16,128]{2,1,0:T(8,128)(2,1)S(1)}, u32[]{:S(2)}, u32[]{:S(2)}) collective-permute-start(bf16[60,16,128]{2,1,0:T(8,128)(2,1)S(1)} %pad_maximum_fusion.mid), channel_id=1, source_target_pairs={{0,16},{8,24},{16,0},{24,8},{32,48},{40,56},{48,32},{56,40},{64,80... | collective-permute-start | bytes 737288 | tf_op jit(solution)/shard_map/ppermute | solution.py:24
  16.1 5.9 %collective-permute-start.5 = (bf16[60,16,128]{2,1,0:T(8,128)(2,1)S(1)}, bf16[60,16,128]{2,1,0:T(8,128)(2,1)S(1)}, u32[]{:S(2)}, u32[]{:S(2)}) collective-permute-start(bf16[60,16,128]{2,1,0:T(8,128)(2,1)S(1)} %pad_maximum_fusion.mid), channel_id=1, source_target_pairs={{8,16},{16,8},{40,48},{48,40},{72,80},{80,72},{104,112},{112,104},... | collective-permute-start | bytes 737288 | tf_op jit(solution)/shard_map/ppermute | solution.py:296
  22.0 1.9 %collective-permute-start.4 = (bf16[60,16,128]{2,1,0:T(8,128)(2,1)S(1)}, bf16[60,16,128]{2,1,0:T(8,128)(2,1)S(1)}, u32[]{:S(2)}, u32[]{:S(2)}) collective-permute-start(bf16[60,16,128]{2,1,0:T(8,128)(2,1)S(1)} %pad_maximum_fusion.mid), channel_id=1, source_target_pairs={{0,8},{8,0},{16,24},{24,16},{32,40},{40,32},{48,56},{56,48},{64,72... | collective-permute-start | bytes 737288 | tf_op jit(solution)/shard_map/ppermute | solution.py:24
  23.9 0.0 collective-permute-done.2.odd2
  23.9 2.4 %collective-permute-start.3 = (bf16[60,16,128]{2,1,0:T(8,128)(2,1)S(1)}, bf16[60,16,128]{2,1,0:T(8,128)(2,1)S(1)}, u32[]{:S(2)}, u32[]{:S(2)}) collective-permute-start(bf16[60,16,128]{2,1,0:T(8,128)(2,1)S(1)} %collective-permute-done.2.odd2), channel_id=1, source_target_pairs={{16,24},{40,32},{48,56},{72,64},{80,88},{104,96},{112,120},{136,12... | collective-permute-start | bytes 737288 | tf_op jit(solution)/shard_map/ppermute | solution.py:298
  26.3 0.2 fusion.1.order2_ref
  26.5 0.0 copy-start
  26.5 0.0 copy-start.1
  26.5 0.0 copy-start.2
  26.5 0.2 fusion.order1_ref
  26.7 0.0 collective-permute-done.6.even2
  26.7 0.0 collective-permute-done.5.cross
  26.7 0.0 collective-permute-done.4.mate
  26.7 0.7 %collective-permute-done.3.relay = bf16[60,16,128]{2,1,0:T(8,128)(2,1)S(1)} collective-permute-done((bf16[60,16,128]{2,1,0:T(8,128)(2,1)S(1)}, bf16[60,16,128]{2,1,0:T(8,128)(2,1)S(1)}, u32[]{:S(2)}, u32[]{:S(2)}) %collective-permute-start.3) | collective-permute-done | bytes 245792 | tf_op jit(solution)/shard_map/ppermute | solution.py:298
  27.5 0.0 copy-done
  27.5 0.0 copy-done.1
  27.5 0.0 copy-done.2
  27.5 3.6 %transport.1 = (bf16[8,4,16,128]{3,2,1,0:T(8,128)(2,1)}, f32[3,4,16,128]{3,2,1,0:T(8,128)}) custom-call(s32[4,2,64]{2,1,0:T(2,128)S(1)} %bitcast.16, s32[4,2,16]{2,1,0:T(2,128)S(1)} %bitcast.17, s32[4,2,16,128]{3,2,1,0:T(8,128)S(1)} %copy-done, bf16[512,512]{1,0:T(8,128)(2,1)S(1)} %fusion.order1_ref, bf16[512,512]{1,0:T(8,128)(2,1)S(1)} %fusion.1.order2_ref, ...), custom_call_target="tpu_custom_call" | custom-call | tf_op jit(solution)/shard_map/transport/pallas_call | solution.py:304
  (3 shorter events, 0.1 us)
Async XLA Ops:
  0.6 9.0 %copy-start.3 = (bf16[8,4,16,128]{3,2,1,0:T(8,128)(2,1)S(1)}, bf16[8,4,16,128]{3,2,1,0:T(8,128)(2,1)}, u32[]{:S(2)}) copy-start(bf16[8,4,16,128]{3,2,1,0:T(8,128)(2,1)} %param.5) | copy-start | bytes 393220
  1.5 4.7 %collective-permute-start = (bf16[8,16,128]{2,1,0:T(8,128)(2,1)S(1)}, bf16[8,16,128]{2,1,0:T(8,128)(2,1)S(1)}, u32[]{:S(2)}, u32[]{:S(2)}) collective-permute-start(bf16[8,16,128]{2,1,0:T(8,128)(2,1)S(1)} %get-tuple-element.4), channel_id=1, source_target_pairs={{0,1},{1,0},{2,3},{3,2},{4,5},{5,4},{6,7},{7,6},{8,9},{9,8},{10,11... | collective-permute-start | bytes 98312 | tf_op jit(solution)/shard_map/ppermute | solution.py:24
  3.8 5.9 %collective-permute-start.1 = (bf16[8,16,128]{2,1,0:T(8,128)(2,1)S(1)}, bf16[8,16,128]{2,1,0:T(8,128)(2,1)S(1)}, u32[]{:S(2)}, u32[]{:S(2)}) collective-permute-start(bf16[8,16,128]{2,1,0:T(8,128)(2,1)S(1)} %get-tuple-element.5), channel_id=1, source_target_pairs={{1,2},{2,1},{3,4},{4,3},{5,6},{6,5},{9,10},{10,9},{11,12},{12,11},... | collective-permute-start | bytes 98312 | tf_op jit(solution)/shard_map/ppermute | solution.py:24
  5.7 4.0 %copy-start.4 = (bf16[3,4,16,128]{3,2,1,0:T(8,128)(2,1)S(1)}, bf16[3,4,16,128]{3,2,1,0:T(8,128)(2,1)}, u32[]{:S(2)}) copy-start(bf16[3,4,16,128]{3,2,1,0:T(8,128)(2,1)} %param.6) | copy-start | bytes 147460
  9.7 14.2 %collective-permute-start.2 = (bf16[60,16,128]{2,1,0:T(8,128)(2,1)S(1)}, bf16[60,16,128]{2,1,0:T(8,128)(2,1)S(1)}, u32[]{:S(2)}, u32[]{:S(2)}) collective-permute-start(bf16[60,16,128]{2,1,0:T(8,128)(2,1)S(1)} %pad_maximum_fusion.mid), channel_id=1, source_target_pairs={{16,32},{24,40},{32,16},{40,24},{48,64},{56,72},{64,48},{72,56},{8... | collective-permute-start | bytes 737288 | tf_op jit(solution)/shard_map/ppermute | solution.py:24
  14.1 12.6 %collective-permute-start.6 = (bf16[60,16,128]{2,1,0:T(8,128)(2,1)S(1)}, bf16[60,16,128]{2,1,0:T(8,128)(2,1)S(1)}, u32[]{:S(2)}, u32[]{:S(2)}) collective-permute-start(bf16[60,16,128]{2,1,0:T(8,128)(2,1)S(1)} %pad_maximum_fusion.mid), channel_id=1, source_target_pairs={{0,16},{8,24},{16,0},{24,8},{32,48},{40,56},{48,32},{56,40},{64,80... | collective-permute-start | bytes 737288 | tf_op jit(solution)/shard_map/ppermute | solution.py:24
  16.1 10.7 %collective-permute-start.5 = (bf16[60,16,128]{2,1,0:T(8,128)(2,1)S(1)}, bf16[60,16,128]{2,1,0:T(8,128)(2,1)S(1)}, u32[]{:S(2)}, u32[]{:S(2)}) collective-permute-start(bf16[60,16,128]{2,1,0:T(8,128)(2,1)S(1)} %pad_maximum_fusion.mid), channel_id=1, source_target_pairs={{8,16},{16,8},{40,48},{48,40},{72,80},{80,72},{104,112},{112,104},... | collective-permute-start | bytes 737288 | tf_op jit(solution)/shard_map/ppermute | solution.py:296
  22.0 4.7 %collective-permute-start.4 = (bf16[60,16,128]{2,1,0:T(8,128)(2,1)S(1)}, bf16[60,16,128]{2,1,0:T(8,128)(2,1)S(1)}, u32[]{:S(2)}, u32[]{:S(2)}) collective-permute-start(bf16[60,16,128]{2,1,0:T(8,128)(2,1)S(1)} %pad_maximum_fusion.mid), channel_id=1, source_target_pairs={{0,8},{8,0},{16,24},{24,16},{32,40},{40,32},{48,56},{56,48},{64,72... | collective-permute-start | bytes 737288 | tf_op jit(solution)/shard_map/ppermute | solution.py:24
  23.9 3.5 %collective-permute-start.3 = (bf16[60,16,128]{2,1,0:T(8,128)(2,1)S(1)}, bf16[60,16,128]{2,1,0:T(8,128)(2,1)S(1)}, u32[]{:S(2)}, u32[]{:S(2)}) collective-permute-start(bf16[60,16,128]{2,1,0:T(8,128)(2,1)S(1)} %collective-permute-done.2.odd2), channel_id=1, source_target_pairs={{16,24},{40,32},{48,56},{72,64},{80,88},{104,96},{112,120},{136,12... | collective-permute-start | bytes 737288 | tf_op jit(solution)/shard_map/ppermute | solution.py:298
  26.5 0.9 %copy-start = (s32[4,2,16,128]{3,2,1,0:T(8,128)S(1)}, s32[4,2,16,128]{3,2,1,0:T(8,128)}, u32[]{:S(2)}) copy-start(s32[4,2,16,128]{3,2,1,0:T(8,128)} %base_ref.1) | copy-start | bytes 196612
  26.5 0.9 %copy-start.1 = (s32[4,64,2]{1,2,0:T(2,128)S(1)}, s32[4,64,2]{1,2,0:T(2,128)}, u32[]{:S(2)}) copy-start(s32[4,64,2]{1,2,0:T(2,128)} %param.9) | copy-start | bytes 6148
  26.5 0.9 %copy-start.2 = (s32[4,16,2]{1,2,0:T(2,128)S(1)}, s32[4,16,2]{1,2,0:T(2,128)}, u32[]{:S(2)}) copy-start(s32[4,16,2]{1,2,0:T(2,128)} %param.7) | copy-start | bytes 1540
